TPU v7x, 256 devices: a whole 4x4x8 slice. The times are simulated.
256 devices in a mesh: cfg: 2 (over core), req: 4 (over y), seq: 32 (over z, x).
Axes of the slice: x: 4, y: 4, z: 8, core: 2. Of those that a mesh axis runs over, the one named last changes fastest.
Arguments:
- patches: float32 [16, 1024, 16], P('req', 'seq'), may hold values from -6 to 6
- noise: float32 [16, 1024, 16], P('req', 'seq'), may hold values from -6 to 6
- timesteps: int32 [16], replicated, may hold values from 50 to 950
- labels: int32 [16], replicated, may hold values from 0 to 999
- lengths: int32 [16], replicated, may hold values from 1 to 1024, 12288 in all
- time_w1: bfloat16 [256, 1152], replicated, may hold values from -0.375 to 0.375
- time_w2: bfloat16 [1152, 1152], replicated, may hold values from -0.1875 to 0.1875
- label_table: bfloat16 [1001, 1152], replicated, may hold values from -5 to 5
- patch_w: bfloat16 [16, 1152], replicated, may hold values from -1.5 to 1.5
- mod_w: bfloat16 [1152, 5760], P(None, ('req', 'seq')), may hold values from -0.1875 to 0.1875
- qkv_w: bfloat16 [1152, 3456], P('req')
- out_w: bfloat16 [1152, 1152], P(None, 'req'), may hold values from -0.1875 to 0.1875
- head_w: bfloat16 [1152, 32], replicated, may hold values from -0.1875 to 0.1875
Outputs:
- guided_update: float32 [16, 1024, 16], P('req', 'seq', 'cfg')
- hidden_norms: float32 [2, 16], P('cfg', 'req')
- max_logits: float32 [2, 16, 16], P('cfg', 'req')
Inputs may be any that keep to these rules, and one draw needn't show every extreme that they name: The lengths of the 16 requests sum to 12288, and the longest has exactly 1024 tokens.
All inputs are finite; a program needn't handle non-finite values.
Results may differ from a plain program's by a relative error of at most 0.0029.
Values may be sent and summed in bfloat16 or wider, within the bound.
A program may use at most 128 MiB of HBM per device.

v0:
```python
import math

import jax
import jax.numpy as jnp
from jax import lax
from jax.sharding import PartitionSpec as P

HEADS = 16
FREQ = 256


norm_eps = 1e-06
masked_score = -1e30
guide_scale = 4.0
plan_offset = 0.008
diffusion_steps = 1000.0


def partner(value, axis, stride):
    mask = 2**stride
    pairs = [(source, source ^ mask) for source in range(lax.axis_size(axis))]
    return lax.ppermute(value, axis, pairs)


def layer_norm(values):
    center = values - jnp.mean(values, axis=-1, keepdims=True)
    spread = jnp.mean(center * center, axis=-1, keepdims=True)
    return center * lax.rsqrt(spread + norm_eps)


def sine_table(places, count, cos_first):
    half = count // 2
    rates = jnp.exp(-math.log(10000.0) * jnp.arange(half, dtype=jnp.float32) / half)
    angles = places.astype(jnp.float32)[:, None] * rates[None, :]
    if cos_first:
        return jnp.concatenate([jnp.cos(angles), jnp.sin(angles)], axis=1)
    return jnp.concatenate([jnp.sin(angles), jnp.cos(angles)], axis=1)


def alpha_bar(steps):
    phase = (steps / diffusion_steps + plan_offset) / (1.0 + plan_offset) * (math.pi / 2.0)
    return jnp.cos(phase) ** 2


def sampler_step(patches, noise, guided, varpart, steps, valid):
    abar = alpha_bar(steps)
    abar_prev = alpha_bar(steps - 1.0)
    beta = 1.0 - abar / abar_prev
    start = (patches - jnp.sqrt(1.0 - abar) * guided) / jnp.sqrt(abar)
    mean = (
        beta * jnp.sqrt(abar_prev) / (1.0 - abar) * start
        + (1.0 - abar_prev) * jnp.sqrt(1.0 - beta) / (1.0 - abar) * patches
    )
    tilde = beta * (1.0 - abar_prev) / (1.0 - abar)
    frac = (varpart + 1.0) * 0.5
    logvar = frac * jnp.log(beta) + (1.0 - frac) * jnp.log(tilde)
    return jnp.where(valid, mean + jnp.exp(0.5 * logvar) * noise, 0.0)


def body(
    patches,
    noise,
    timesteps,
    labels,
    lengths,
    time_w1,
    time_w2,
    label_table,
    patch_w,
    mod_w,
    qkv_w,
    out_w,
    head_w,
):
    req_dev, slot_dev, patch_in = patches.shape
    width = patch_w.shape[1]
    head_dim = width // HEADS
    seq_total = slot_dev * lax.axis_size("seq")
    copy_index = lax.axis_index("cfg")
    is_cond = copy_index == 0
    tfreq = sine_table(timesteps, FREQ, True).astype(jnp.bfloat16)
    time_hidden = jax.nn.silu(jnp.dot(tfreq, time_w1, preferred_element_type=jnp.float32)).astype(
        jnp.bfloat16
    )
    time_embed = jnp.dot(time_hidden, time_w2, preferred_element_type=jnp.float32)
    label_rows = label_table.shape[0]
    label_used = jnp.where(is_cond, labels, label_rows - 1)
    one_hot = (label_used[:, None] == jnp.arange(label_rows, dtype=jnp.int32)[None, :]).astype(
        jnp.bfloat16
    )
    cond = time_embed + jnp.dot(one_hot, label_table, preferred_element_type=jnp.float32)
    cond_act = jax.nn.silu(cond).astype(jnp.bfloat16)
    mod_part = jnp.dot(cond_act, mod_w, preferred_element_type=jnp.float32)
    mod_all = lax.all_gather(mod_part, ("req", "seq"), axis=1, tiled=True)
    first_req = lax.axis_index("req") * req_dev
    modulation = lax.dynamic_slice_in_dim(mod_all, first_req, req_dev, 0).reshape(req_dev, 5, width)
    my_lengths = lax.dynamic_slice_in_dim(lengths, first_req, req_dev, 0)
    my_steps = lax.dynamic_slice_in_dim(timesteps, first_req, req_dev, 0)
    shift1 = modulation[:, 0][:, None, :]
    scale1 = modulation[:, 1][:, None, :]
    gate1 = modulation[:, 2][:, None, :]
    shift2 = modulation[:, 3][:, None, :]
    scale2 = modulation[:, 4][:, None, :]
    slot_pos = lax.axis_index("seq") * slot_dev + jnp.arange(slot_dev, dtype=jnp.int32)
    position = sine_table(slot_pos, width, False)
    token_rows = req_dev * slot_dev
    embedded = jnp.dot(
        patches.astype(jnp.bfloat16).reshape(token_rows, patch_in),
        patch_w,
        preferred_element_type=jnp.float32,
    )
    hidden0 = embedded.reshape(req_dev, slot_dev, width) + position[None, :, :]
    normed1 = (layer_norm(hidden0) * (1.0 + scale1) + shift1).astype(jnp.bfloat16)
    normed_rows = normed1.reshape(token_rows, width)
    projected = jnp.dot(
        normed_rows,
        lax.all_gather(qkv_w, "req", axis=0, tiled=True),
        preferred_element_type=jnp.float32,
    )
    query = projected[:, :width].astype(jnp.bfloat16).reshape(req_dev, slot_dev, HEADS, head_dim)
    keys_local = (
        projected[:, width : 2 * width].astype(jnp.bfloat16).reshape(req_dev, slot_dev, width)
    )
    values_local = projected[:, 2 * width :].astype(jnp.bfloat16).reshape(req_dev, slot_dev, width)
    inv_root = 1.0 / math.sqrt(head_dim)
    keys_all, values_all = (
        lax.all_gather(keys_local, "seq", axis=1, tiled=True),
        lax.all_gather(values_local, "seq", axis=1, tiled=True),
    )
    keys_heads = keys_all.reshape(req_dev, seq_total, HEADS, head_dim)
    values_heads = values_all.reshape(req_dev, seq_total, HEADS, head_dim)
    scores = (
        jnp.einsum("rqhd,rkhd->rhqk", query, keys_heads, preferred_element_type=jnp.float32)
        * inv_root
    )
    key_ok = (jnp.arange(seq_total, dtype=jnp.int32)[None, :] < my_lengths[:, None])[
        :, None, None, :
    ]
    scores = jnp.where(key_ok, scores, masked_score)
    row_max = jnp.max(scores, axis=3)
    expo = jnp.where(key_ok, jnp.exp(scores - row_max[..., None]), 0.0)
    total = jnp.sum(expo, axis=3)
    summed = jnp.einsum(
        "rhqk,rkhd->rqhd",
        expo.astype(jnp.bfloat16),
        values_heads,
        preferred_element_type=jnp.float32,
    )
    mixed = (
        (summed / jnp.transpose(total, (0, 2, 1))[..., None])
        .astype(jnp.bfloat16)
        .reshape(token_rows, width)
    )
    attended = jnp.dot(
        mixed, lax.all_gather(out_w, "req", axis=1, tiled=True), preferred_element_type=jnp.float32
    )
    hidden1 = hidden0 + gate1 * attended.reshape(req_dev, slot_dev, width)
    query_ok = slot_pos[None, :] < my_lengths[:, None]
    squares = jnp.sum(jnp.where(query_ok[:, :, None], hidden1 * hidden1, 0.0), axis=(1, 2))
    local_top = jnp.max(jnp.where(query_ok[:, None, :], row_max, masked_score), axis=2)
    total_squares = lax.psum(squares, "seq")
    top = lax.pmax(local_top, "seq")
    norm_values = jnp.sqrt(total_squares / (my_lengths.astype(jnp.float32) * width))
    normed2 = (layer_norm(hidden1) * (1.0 + scale2) + shift2).astype(jnp.bfloat16)
    prediction = jnp.dot(
        normed2.reshape(token_rows, width), head_w, preferred_element_type=jnp.float32
    ).reshape(req_dev, slot_dev, head_w.shape[1])
    other = partner(prediction, "cfg", 0)
    pred_cond = jnp.where(is_cond, prediction, other)
    pred_uncond = jnp.where(is_cond, other, prediction)
    eps_cond = pred_cond[..., :patch_in]
    eps_uncond = pred_uncond[..., :patch_in]
    guided = eps_uncond + guide_scale * (eps_cond - eps_uncond)
    varpart = pred_cond[..., patch_in:]
    channel_half = patch_in // lax.axis_size("cfg")
    channel_first = copy_index * channel_half

    def own_channels(values):
        return lax.dynamic_slice_in_dim(values, channel_first, channel_half, 2)

    steps = my_steps.astype(jnp.float32)[:, None, None]
    guided_update = sampler_step(
        own_channels(patches),
        own_channels(noise),
        own_channels(guided),
        own_channels(varpart),
        steps,
        query_ok[:, :, None],
    )
    return (guided_update, norm_values[None, :], top[None, :, :])


def solution(mesh):
    in_specs = (
        P("req", "seq", None),
        P("req", "seq", None),
        P(),
        P(),
        P(),
        P(),
        P(),
        P(),
        P(),
        P(None, ("req", "seq")),
        P("req", None),
        P(None, "req"),
        P(),
    )
    out_specs = (P("req", "seq", "cfg"), P("cfg", "req"), P("cfg", "req", None))
    return jax.shard_map(body, mesh=mesh, in_specs=in_specs, out_specs=out_specs, check_vma=False)
```

profile of v0, /device:TPU:2, one launch (start us, length us, event | category | flops | bytes accessed | tf_op | source)
XLA Modules:
  0.0 769.9 jit_solution(16310428311648811346)
XLA Ops:
  7.2 0.7 all-gather.6.cloned.1.call-update
  8.0 0.7 convert_element_type.45
  8.7 0.7 broadcast_select_fusion.1
  9.3 0.1 fusion.43
  9.5 1.7 fusion.27
  11.1 2.3 convolution_bitcast_fusion
  13.4 348.6 %all-gather = f32[128,45,16]{1,2,0:T(8,128)S(1)} all-gather(f32[1,45,16]{1,2,0:T(8,128)S(1)} %convolution_bitcast_fusion), channel_id=1, replica_groups=mesh['cfg'=2,'req'=4,'seq'=32] {'req','seq'}, dimensions={0}, use_global_device_ids=true | all-gather | bytes 371520 | tf_op jit(solution)/shard_map/all_gather | solution.py:94
  362.0 0.3 copy.24
  362.3 0.5 reshape.193
  363.0 0.4 multiply_sine_fusion
  363.3 0.1 pad_maximum_fusion
  363.4 0.3 fusion.67
  363.8 0.2 multiply_reduce_fusion.1
  364.0 0.1 slice_add_fusion
  364.1 0.2 add_convert_fusion.1
  364.4 4.6 convolution_convert_fusion
  369.0 0.9 fusion.65
  370.0 0.7 all-gather.8.cloned.1.call-update
  370.7 0.2 all-gather.12.cloned.1.call-start
  370.9 0.3 all-gather.12.cloned.1.call-update
  371.2 0.1 dynamic_slice.21
  371.3 0.6 copy.43
  371.9 0.1 multiply_divide_fusion.3
  372.1 0.1 broadcast_compare_fusion
  372.1 0.6 fusion.63
  372.8 0.1 iota_compare_fusion.3
  372.8 0.6 copy_bitcast_fusion
  373.5 0.9 reshape.189
  374.4 94.2 %all-gather.10.cloned.1.call-done = bf16[4,1024,1152]{2,1,0:T(8,128)(2,1)} async-done(((bf16[4,32,1152]{2,1,0:T(8,128)(2,1)}), bf16[4,1024,1152]{2,1,0:T(8,128)(2,1)}) %all-gather.10.cloned.1.call-update) | async-done | bytes 9437200 | tf_op jit(solution)/shard_map/all_gather | solution.py:127
  468.6 12.7 %copy.26 = bf16[4,1024,1152]{1,2,0:T(8,128)(2,1)} copy(bf16[4,1024,1152]{2,1,0:T(8,128)(2,1)} %all-gather.10.cloned.1.call-done) | data formatting | bytes 18874368 | tf_op jit(solution)/shard_map/all_gather | solution.py:127
  481.3 90.2 %all-gather.8.cloned.1.call-done = bf16[4,1024,1152]{2,1,0:T(8,128)(2,1)} async-done(((bf16[4,32,1152]{2,1,0:T(8,128)(2,1)}), bf16[4,1024,1152]{2,1,0:T(8,128)(2,1)}) %all-gather.8.cloned.1.call-update) | async-done | bytes 9437200 | tf_op jit(solution)/shard_map/all_gather | solution.py:128
  571.4 12.7 %copy.25 = bf16[4,1024,1152]{1,2,0:T(8,128)(2,1)} copy(bf16[4,1024,1152]{2,1,0:T(8,128)(2,1)} %all-gather.8.cloned.1.call-done) | data formatting | bytes 18874368 | tf_op jit(solution)/shard_map/all_gather | solution.py:128
  584.2 5.3 fusion
  589.5 3.2 copy-done.2
  592.7 2.4 fusion.1
  595.1 10.0 %divide_convert_fusion = bf16[4,32,16,72]{3,1,2,0:T(8,128)(2,1)} fusion(bf16[4,1024,16,72]{1,3,2,0:T(8,128)(2,1)} %bitcast.61, f32[4,16,32,1024]{3,2,1,0:T(8,128)} %copy-done.2, f32[4,16,32]{2,1,0:T(8,128)S(1)} %get-tuple-element.32, pred[4,1024]{1,0:T(4,128)(4,1)S(1)} %iota_compare_fusion.3, f32[4,32,16]{1,2,0:T(8,128)S(1)} %bitcast.66), kind=kOutput, calls=%fused_computation.20 | convolution fusion | flops 312770560 | bytes 18141184 | tf_op jit(solution)/shard_map/rhqk,rkhd->rqhd/dot_general | solution.py:143
  605.1 2.0 copy.28
  607.1 1.6 dot_general.40
  608.6 0.8 all-gather.12.cloned.1.call-done
  609.4 2.8 fusion.68
  612.2 0.3 select_reduce_fusion
  612.5 1.4 fusion.25
  613.9 0.1 collective-permute-start
  614.0 71.1 %psum.7 = f32[4]{0:T(128)S(1)} all-reduce(f32[4]{0:T(128)S(1)} %get-tuple-element.3), channel_id=1, replica_groups=mesh['cfg'=2,'req'=4,'seq'=32] {'seq'}, use_global_device_ids=true, to_apply=%region_7.8 | all-reduce | flops 4 | bytes 32 | tf_op jit(solution)/shard_map/psum | solution.py:161
  685.1 1.3 sqrt_bitcast_fusion
  686.3 0.8 select_reduce_fusion.1
  687.2 74.7 %pmax.7 = f32[1,4,16]{2,1,0:T(4,128)} all-reduce(f32[1,4,16]{2,1,0:T(4,128)S(1)} %bitcast.67), channel_id=1, replica_groups=mesh['cfg'=2,'req'=4,'seq'=32] {'seq'}, use_global_device_ids=true, to_apply=%region_9.10 | all-reduce | flops 64 | bytes 512 | tf_op jit(solution)/shard_map/pmax | solution.py:162
  761.9 1.5 fusion.42
  (35 shorter events, 0.3 us)
Async XLA Ops:
  7.2 2.3 copy-start
  7.2 356.2 %copy-start.4 = (f32[4,32,16]{1,2,0:T(8,128)S(1)}, f32[4,32,16]{1,2,0:T(8,128)}, u32[]{:S(2)}) copy-start(f32[4,32,16]{1,2,0:T(8,128)} %param.13) | copy-start | bytes 24580
  7.2 356.2 %copy-start.5 = (bf16[16,1152]{1,0:T(8,128)(2,1)S(1)}, bf16[16,1152]{1,0:T(8,128)(2,1)}, u32[]{:S(2)}) copy-start(bf16[16,1152]{1,0:T(8,128)(2,1)} %param.21) | copy-start | bytes 110596
  7.2 357.1 %all-gather.6.cloned.1.call-start = ((), (), s32[]{:S(2)}) async-start(), calls=%async_computation | async-start | bytes 9953280 | tf_op jit(solution)/shard_map/all_gather | solution.py:117
  7.9 460.7 %all-gather.10.cloned.1.call-start = ((), (), s32[]{:S(2)}) async-start(), calls=%async_computation.2 | async-start | bytes 9732096 | tf_op jit(solution)/shard_map/all_gather | solution.py:127
  364.4 6.9 copy-start.7
  364.4 7.6 copy-start.6
  369.9 201.5 %all-gather.8.cloned.1.call-start = ((), (), s32[]{:S(2)}) async-start(), calls=%async_computation.1 | async-start | bytes 9732096 | tf_op jit(solution)/shard_map/all_gather | solution.py:128
  370.7 238.8 %all-gather.12.cloned.1.call-start = ((), (), s32[]{:S(2)}) async-start(), calls=%async_computation.3 | async-start | bytes 3317760 | tf_op jit(solution)/shard_map/all_gather | solution.py:155
  589.4 3.2 copy-start.2
  589.5 15.6 %copy-start.3 = (f32[4,16,32]{2,1,0:T(8,128)}, f32[4,16,32]{2,1,0:T(8,128)S(1)}, u32[]{:S(2)}) copy-start(f32[4,16,32]{2,1,0:T(8,128)S(1)} %get-tuple-element.32) | copy-start | bytes 24580
  595.1 168.3 %copy-start.1 = (bf16[1152,1152]{1,0:T(8,128)(2,1)S(1)}, bf16[1152,1152]{1,0:T(8,128)(2,1)}, u32[]{:S(2)}) copy-start(bf16[1152,1152]{1,0:T(8,128)(2,1)} %param.19) | copy-start | bytes 7962628
  613.9 148.0 %collective-permute-start = (f32[4,32,32]{1,2,0:T(8,128)S(1)}, f32[4,32,32]{1,2,0:T(8,128)S(1)}, u32[]{:S(2)}, u32[]{:S(2)}) collective-permute-start(f32[4,32,32]{1,2,0:T(8,128)S(1)} %fusion.25), channel_id=1, source_target_pairs={{0,128},{128,0},{1,129},{129,1},{2,130},{130,2},{3,131},{131,3},{4... | collective-permute-start | bytes 49160 | tf_op jit(solution)/shard_map/ppermute | solution.py:22
Sparse Core Ops, SparseCore 0:
  9.8 85.0 all-gather.5
  370.0 98.5 all-gather.9
  471.2 100.1 all-gather.7
  573.1 36.3 all-gather.11
where the time goes:
time: 771 us; the launch traced here: 770 us
  blocking collectives  494 us (64%)
  waiting for transfers between devices  187 us (24%)
  local copies, waits for them, and re-layouts  36.3 us (5%)
  matrix products  28.3 us (4%)
  between operations  14 us (2%)
  other arithmetic  9.52 us (1%)
    all_gather x1, blocking collectives, body(): mod_all = lax.all_gather(mod_part, ('req', 'seq'), axis=1, tiled=True)  349 us
    all_gather x1, waiting for transfers between devices, body(): lax.all_gather(keys_local, 'seq', axis=1, tiled=True)  94.2 us
    all_gather x1, waiting for transfers between devices, body(): lax.all_gather(values_local, 'seq', axis=1, tiled=True)  90.2 us
    pmax x1, blocking collectives, body(): top = lax.pmax(local_top, 'seq')  74.7 us
    psum x1, blocking collectives, body(): total_squares = lax.psum(squares, 'seq')  71.1 us
  transfers between devices with their start and end apart: 5, of which 3 were waited for; matrix products, arithmetic and copies ran while one was open for 8% of the time, Pallas kernels for 0%

commit v1 on v0

v1 whole, which is shorter than its diff:
```python
import math

import jax
import jax.numpy as jnp
import numpy as np
from jax import lax
from jax.experimental import pallas as pl
from jax.experimental.pallas import tpu as pltpu
from jax.sharding import PartitionSpec as P

HEADS = 16
FREQ = 256
D = 1152
SEQ_TOTAL = 1024
NSEQ = 32
NREQ = 4
NDEV = NSEQ * NREQ
GROUP = 8
SLOT = 32
BLK = 128
WIN = 256
PAIR = 144
HEAD_DIM = 72
ROWS = 288
HALF = 144
MODC = 45
MESH = pl.DeviceIdType.MESH

norm_eps = 1e-06
masked_score = -1e30
guide_scale = 4.0
plan_offset = 0.008
diffusion_steps = 1000.0
INV_ROOT = 1.0 / math.sqrt(HEAD_DIM)
EXP_SCALE = INV_ROOT * math.log2(math.e)


def time_table(places):
    half = FREQ // 2
    rates = jnp.exp(-math.log(10000.0) * jnp.arange(half, dtype=jnp.float32) / half)
    angles = places.astype(jnp.float32)[:, None] * rates[None, :]
    return jnp.concatenate([jnp.cos(angles), jnp.sin(angles)], axis=1)


def position_factors():
    half = D // 2
    rates = np.exp(-math.log(10000.0) * np.arange(half) / half)
    coarse = (SLOT * np.arange(NSEQ))[:, None] * rates[None, :]
    fine = np.arange(SLOT)[:, None] * rates[None, :]
    sc, cc, sf, cf = np.sin(coarse), np.cos(coarse), np.sin(fine), np.cos(fine)
    p1 = np.concatenate([sc, cc], axis=1)[:, None, :]
    p2 = np.concatenate([cc, -sc], axis=1)[:, None, :]
    q1 = np.concatenate([cf, cf], axis=1)
    q2 = np.concatenate([sf, sf], axis=1)
    return [jnp.asarray(t.astype(np.float32)) for t in (p1, p2, q1, q2)]


def alpha_bar(steps):
    phase = (steps / diffusion_steps + plan_offset) / (1.0 + plan_offset) * (math.pi / 2.0)
    return jnp.cos(phase) ** 2


def sampler_step(patches, noise, guided, varpart, steps, valid):
    abar = alpha_bar(steps)
    abar_prev = alpha_bar(steps - 1.0)
    beta = 1.0 - abar / abar_prev
    start = (patches - jnp.sqrt(1.0 - abar) * guided) / jnp.sqrt(abar)
    mean = (
        beta * jnp.sqrt(abar_prev) / (1.0 - abar) * start
        + (1.0 - abar_prev) * jnp.sqrt(1.0 - beta) / (1.0 - abar) * patches
    )
    tilde = beta * (1.0 - abar_prev) / (1.0 - abar)
    frac = (varpart + 1.0) * 0.5
    logvar = frac * jnp.log(beta) + (1.0 - frac) * jnp.log(tilde)
    return jnp.where(valid, mean + jnp.exp(0.5 * logvar) * noise, 0.0)


def layer_norm(values):
    center = values - jnp.mean(values, axis=-1, keepdims=True)
    spread = jnp.mean(center * center, axis=-1, keepdims=True)
    return center * lax.rsqrt(spread + norm_eps)


def kernel(
    len_ref, patches_ref, modp_ref, qkv_hbm, outw_hbm, headw_ref, patchw_ref, p1_ref, p2_ref, q1_ref, q2_ref,
    pred_out, stat_out,
    pb, patch_all, mod_all, mod_rows, wbuf, outbuf, qbuf, kbuf, vbuf, mbuf, mixin, att, predsend, pred_in, stat_send, stat_in, top,
    mod_s, mod_r, pat_s, pat_r, w_s, w_r, wl, wf_s, wf_r, o_s, o_r, ol, of_s, of_r, mx_s, mx_r, pr_s, pr_r, st_s, st_r,
):
    g = lax.axis_index("cfg")
    y = lax.axis_index("req")
    s = lax.axis_index("seq")
    other = 1 - g
    me = y * NSEQ + s
    q = lax.div(s, GROUP)
    j = lax.rem(s, GROUP)

    def remote(src, dst, ssem, rsem, dev):
        return pltpu.make_async_remote_copy(
            src_ref=src, dst_ref=dst, send_sem=ssem, recv_sem=rsem, device_id=dev, device_id_type=MESH
        )

    bar = pltpu.get_barrier_semaphore()

    def greet(k, _):
        d = lax.rem(me + k, NDEV)
        pl.semaphore_signal(bar, inc=1, device_id=(g, lax.div(d, NSEQ), lax.rem(d, NSEQ)), device_id_type=MESH)
        return 0

    lax.fori_loop(1, NDEV, greet, 0)
    for qq in range(NREQ):
        pl.semaphore_signal(bar, inc=1, device_id=(other, y, qq * GROUP + lax.div(s, NREQ)), device_id_type=MESH)
    pl.semaphore_signal(bar, inc=1, device_id=(other, y, s), device_id_type=MESH)

    pb[...] = patches_ref[...].astype(jnp.bfloat16)
    col = pl.multiple_of(j * BLK, BLK)
    local_w = []
    for kind in range(3):
        c = pltpu.make_async_copy(
            qkv_hbm.at[:, pl.ds(pl.multiple_of(kind * D + col, BLK), WIN)],
            wbuf.at[kind, pl.ds(pl.multiple_of(ROWS * y, 16), ROWS), :],
            wl.at[kind],
        )
        c.start()
        local_w.append(c)
    local_o = pltpu.make_async_copy(outw_hbm, outbuf.at[y], ol)
    local_o.start()
    pl.semaphore_wait(bar, NDEV - 1 + NREQ + 1)

    def send_mod(k, _):
        d = lax.rem(me + k, NDEV)
        dy, dq = lax.div(d, NSEQ), lax.rem(d, NSEQ)
        row = dy * NREQ + lax.div(dq, GROUP)
        remote(modp_ref.at[row], mod_all.at[me], mod_s, mod_r, (g, dy, dq)).start()
        return 0

    lax.fori_loop(1, NDEV, send_mod, 0)

    def send_patch(k, _):
        d = lax.rem(s + k, NSEQ)
        remote(pb.at[lax.div(d, GROUP)], patch_all.at[s], pat_s, pat_r, (g, y, d)).start()
        return 0

    lax.fori_loop(1, NSEQ, send_patch, 0)

    w_copies = []
    for dy in range(1, NREQ):
        ty = lax.rem(y + dy, NREQ)
        for kind in range(3):
            c = remote(
                qkv_hbm.at[pl.ds(pl.multiple_of(HALF * g, 16), HALF), pl.ds(pl.multiple_of(kind * D + col, BLK), WIN)],
                wbuf.at[kind, pl.ds(pl.multiple_of(ROWS * y + HALF * g, 16), HALF), :],
                w_s.at[dy - 1, kind],
                w_r.at[dy - 1, kind],
                (g, ty, s),
            )
            c.start()
            w_copies.append((dy, c))

    mod_all[me] = modp_ref[y * NREQ + q]
    patch_all[s] = pb[q]

    w_forwards = []
    for dy in range(1, NREQ):
        for dd, c in w_copies:
            if dd == dy:
                c.wait_recv()
        sy = lax.rem(y + NREQ - dy, NREQ)
        part = wbuf.at[:, pl.ds(pl.multiple_of(ROWS * sy + HALF * g, 16), HALF), :]
        f = remote(part, part, wf_s.at[dy - 1], wf_r.at[dy - 1], (other, y, s))
        f.start()
        w_forwards.append(f)

    pltpu.make_async_copy(mod_all.at[pl.ds(0, NDEV - 1)], mod_all.at[pl.ds(0, NDEV - 1)], mod_r).wait()

    o_copies = []
    for dy in range(1, NREQ):
        ty = lax.rem(y + dy, NREQ)
        rows = pl.ds(pl.multiple_of((D // 2) * g, 16), D // 2)
        c = remote(outw_hbm.at[rows, :], outbuf.at[y, rows, :], o_s.at[dy - 1], o_r.at[dy - 1], (g, ty, s))
        c.start()
        o_copies.append(c)

    lane_row = lax.broadcasted_iota(jnp.int32, (1, BLK), 1)
    for tile in range(5 * D // BLK):
        first = (tile * BLK) // MODC
        last = (tile * BLK + BLK - 1) // MODC
        value = None
        for source in range(first, last + 1):
            at = source * MODC - tile * BLK
            piece = mod_all[source]
            if at % BLK:
                piece = pltpu.roll(piece, at % BLK, 1)
            value = piece if value is None else jnp.where(lane_row >= at, piece, value)
        mod_rows[tile // 9, :, (tile % 9) * BLK : (tile % 9 + 1) * BLK] = value

    length = len_ref[y * NREQ + q]
    pltpu.make_async_copy(patch_all.at[pl.ds(0, NSEQ - 1)], patch_all.at[pl.ds(0, NSEQ - 1)], pat_r).wait()
    for f in w_forwards:
        f.wait_recv()
    for c in local_w:
        c.wait()

    lane = lax.broadcasted_iota(jnp.int32, (1, WIN), 1)
    low = j * 16
    in_a = (lane >= low) & (lane < low + HEAD_DIM)
    in_b = (lane >= low + HEAD_DIM) & (lane < low + PAIR)
    spare = lane == lax.rem(low + PAIR, WIN)

    def embed(first_source, count):
        x = patch_all[pl.ds(first_source, count)].reshape(count * SLOT, 16)
        h = jnp.dot(x, patchw_ref[...], preferred_element_type=jnp.float32)
        places = [
            p1_ref[first_source + i] * q1_ref[...] + p2_ref[first_source + i] * q2_ref[...] for i in range(count)
        ]
        return h + jnp.concatenate(places, axis=0)

    def project(b, _):
        h = embed(b * 8, 8)
        normed = (layer_norm(h) * (1.0 + mod_rows[1]) + mod_rows[0]).astype(jnp.bfloat16)
        rows = pl.ds(pl.multiple_of(b * 256, 256), 256)
        qbuf[rows, :] = jnp.dot(normed, wbuf[0], preferred_element_type=jnp.float32).astype(jnp.bfloat16)
        keys = jnp.dot(normed, wbuf[1], preferred_element_type=jnp.float32)
        place = b * 256 + lax.broadcasted_iota(jnp.int32, (256, 1), 0)
        bias = jnp.where(place < length, 0.0, masked_score)
        kbuf[rows, :] = jnp.where(spare, bias, keys).astype(jnp.bfloat16)
        vbuf[rows, :] = jnp.dot(normed, wbuf[2], preferred_element_type=jnp.float32).astype(jnp.bfloat16)
        return 0

    lax.fori_loop(0, 4, project, 0)

    top[...] = jnp.full_like(top, masked_score)

    def attend(k, _):
        b = lax.rem(j + k, GROUP)
        rows = pl.ds(pl.multiple_of(b * BLK, BLK), BLK)
        query = qbuf[rows, :].astype(jnp.float32)
        live = b * BLK + lax.broadcasted_iota(jnp.int32, (BLK, 1), 0) < length
        mixed = jnp.zeros((BLK, WIN), jnp.float32)
        for head, inside in enumerate((in_a, in_b)):
            mine = jnp.where(inside, query, jnp.where(spare, 1.0, 0.0)).astype(jnp.bfloat16)
            raw = lax.dot_general(mine, kbuf[...], (((1,), (1,)), ((), ())), preferred_element_type=jnp.float32)
            peak = jnp.max(raw, axis=1, keepdims=True)
            expo = jnp.exp2((raw - peak) * EXP_SCALE)
            total = jnp.sum(expo, axis=1, keepdims=True)
            summed = jnp.dot(expo.astype(jnp.bfloat16), vbuf[...], preferred_element_type=jnp.float32)
            mixed = jnp.where(inside, summed * (1.0 / total), mixed)
            best = jnp.max(jnp.where(live, peak, masked_score), axis=0, keepdims=True)
            top[head] = jnp.maximum(top[head], best)
        mbuf[b] = mixed.astype(jnp.bfloat16)

        @pl.when(k < GROUP)
        def _():
            remote(mbuf.at[b], mixin.at[j], mx_s, mx_r, (g, y, q * GROUP + b)).start()

        return 0

    lax.fori_loop(1, GROUP + 1, attend, 0)
    mixin[j] = mbuf[j]

    o_forwards = []
    for dy in range(1, NREQ):
        o_copies[dy - 1].wait_recv()
        sy = lax.rem(y + NREQ - dy, NREQ)
        part = outbuf.at[sy, pl.ds(pl.multiple_of((D // 2) * g, 16), D // 2), :]
        f = remote(part, part, of_s.at[dy - 1], of_r.at[dy - 1], (other, y, s))
        f.start()
        o_forwards.append(f)
    hidden0 = embed(j * 4, 4)
    local_o.wait()
    for f in o_forwards:
        f.wait_recv()
    pltpu.make_async_copy(mixin.at[pl.ds(0, GROUP - 1)], mixin.at[pl.ds(0, GROUP - 1)], mx_r).wait()

    pieces = []
    for part in range(NREQ):
        acc = jnp.zeros((BLK, ROWS), jnp.float32)
        for pair in range(GROUP):
            acc += jnp.dot(
                mixin[pair], outbuf[part, pair * BLK : pair * BLK + WIN, :], preferred_element_type=jnp.float32
            )
        pieces.append(acc)
    attended = jnp.concatenate(pieces, axis=1)
    hidden1 = hidden0 + mod_rows[2] * attended
    place = j * BLK + lax.broadcasted_iota(jnp.int32, (BLK, 1), 0)
    squares = jnp.sum(jnp.sum(jnp.where(place < length, hidden1 * hidden1, 0.0), axis=1, keepdims=True), axis=0, keepdims=True)
    stat = jnp.where(lane_row == 0, squares, jnp.where(lane_row == 1, top[0], top[1]) * INV_ROOT)
    stat_send[...] = stat

    def send_stat(k, _):
        d = lax.rem(s + k, NSEQ)
        remote(stat_send, stat_in.at[s], st_s, st_r, (g, y, d)).start()
        return 0

    lax.fori_loop(1, NSEQ, send_stat, 0)
    stat_in[s] = stat

    normed2 = (layer_norm(hidden1) * (1.0 + mod_rows[4]) + mod_rows[3]).astype(jnp.bfloat16)
    prediction = jnp.dot(normed2, headw_ref[...], preferred_element_type=jnp.float32)
    predsend[...] = prediction.reshape(NREQ, SLOT, 32)
    slot = g * NREQ + q
    p_copies = []
    for i in range(NREQ):
        for gg in range(2):
            ts = j * NREQ + i
            self_copy = (ts == s) & (g == gg)
            c = remote(predsend.at[i], pred_in.at[slot], pr_s.at[i * 2 + gg], pr_r, (gg, y, ts))
            p_copies.append((self_copy, c))

            @pl.when(jnp.logical_not(self_copy))
            def _():
                c.start()

            @pl.when(self_copy)
            def _():
                pltpu.make_async_copy(predsend.at[i], pred_in.at[slot], pr_r).start()

    pltpu.make_async_copy(pred_in, pred_in, pr_r).wait()
    pltpu.make_async_copy(stat_in.at[pl.ds(0, NSEQ - 1)], stat_in.at[pl.ds(0, NSEQ - 1)], st_r).wait()
    pred_out[...] = pred_in[...]
    stat_out[...] = stat_in[...]

    pltpu.make_async_copy(mod_all.at[pl.ds(0, NDEV - 1)], mod_all.at[pl.ds(0, NDEV - 1)], mod_s).wait()
    pltpu.make_async_copy(patch_all.at[pl.ds(0, NSEQ - 1)], patch_all.at[pl.ds(0, NSEQ - 1)], pat_s).wait()
    pltpu.make_async_copy(mixin.at[pl.ds(0, GROUP - 1)], mixin.at[pl.ds(0, GROUP - 1)], mx_s).wait()
    pltpu.make_async_copy(stat_in.at[pl.ds(0, NSEQ - 1)], stat_in.at[pl.ds(0, NSEQ - 1)], st_s).wait()
    for _, c in w_copies:
        c.wait_send()
    for c in w_forwards + o_copies + o_forwards:
        c.wait_send()
    for self_copy, c in p_copies:

        @pl.when(jnp.logical_not(self_copy))
        def _():
            c.wait_send()


def body(
    patches, noise, timesteps, labels, lengths, time_w1, time_w2, label_table, patch_w, mod_w, qkv_w, out_w, head_w
):
    copy_index = lax.axis_index("cfg")
    is_cond = copy_index == 0
    tfreq = time_table(timesteps).astype(jnp.bfloat16)
    time_hidden = jax.nn.silu(jnp.dot(tfreq, time_w1, preferred_element_type=jnp.float32)).astype(jnp.bfloat16)
    time_embed = jnp.dot(time_hidden, time_w2, preferred_element_type=jnp.float32)
    label_rows = label_table.shape[0]
    label_used = jnp.where(is_cond, labels, label_rows - 1)
    one_hot = (label_used[:, None] == jnp.arange(label_rows, dtype=jnp.int32)[None, :]).astype(jnp.bfloat16)
    cond = time_embed + jnp.dot(one_hot, label_table, preferred_element_type=jnp.float32)
    cond_act = jax.nn.silu(cond).astype(jnp.bfloat16)
    mod_part = jnp.dot(cond_act, mod_w, preferred_element_type=jnp.float32)
    modp = jnp.pad(mod_part, ((0, 0), (0, BLK - MODC))).reshape(16, 1, BLK)

    vmem = pl.BlockSpec(memory_space=pltpu.VMEM)
    hbm = pl.BlockSpec(memory_space=pl.ANY)
    bf, f32 = jnp.bfloat16, jnp.float32
    dma = pltpu.SemaphoreType.DMA
    pred, stats = pl.pallas_call(
        kernel,
        out_shape=(
            jax.ShapeDtypeStruct((8, SLOT, 32), f32),
            jax.ShapeDtypeStruct((NSEQ, 1, BLK), f32),
        ),
        in_specs=[pl.BlockSpec(memory_space=pltpu.SMEM), vmem, vmem, hbm, hbm, vmem, vmem, vmem, vmem, vmem, vmem],
        out_specs=(vmem, vmem),
        scratch_shapes=[
            pltpu.VMEM((4, SLOT, 16), bf),
            pltpu.VMEM((NSEQ, SLOT, 16), bf),
            pltpu.VMEM((NDEV, 1, BLK), f32),
            pltpu.VMEM((5, 1, D), f32),
            pltpu.VMEM((3, D, WIN), bf),
            pltpu.VMEM((NREQ, D, ROWS), bf),
            pltpu.VMEM((SEQ_TOTAL, WIN), bf),
            pltpu.VMEM((SEQ_TOTAL, WIN), bf),
            pltpu.VMEM((SEQ_TOTAL, WIN), bf),
            pltpu.VMEM((GROUP, BLK, WIN), bf),
            pltpu.VMEM((GROUP, BLK, WIN), bf),
            pltpu.VMEM((BLK, D), f32),
            pltpu.VMEM((4, SLOT, 32), f32),
            pltpu.VMEM((8, SLOT, 32), f32),
            pltpu.VMEM((1, BLK), f32),
            pltpu.VMEM((NSEQ, 1, BLK), f32),
            pltpu.VMEM((2, 1, 1), f32),
            dma, dma, dma, dma,
            dma((3, 3)), dma((3, 3)), dma((3,)), dma((3,)), dma((3,)),
            dma((3,)), dma((3,)), dma, dma((3,)), dma((3,)),
            dma, dma, dma((8,)), dma, dma, dma,
        ],
        compiler_params=pltpu.CompilerParams(
            collective_id=0, has_side_effects=True, vmem_limit_bytes=56 * 1024 * 1024
        ),
        name="guided_block",
    )(lengths, patches, modp, qkv_w, out_w, head_w, patch_w, *position_factors())

    first_req = lax.axis_index("req") * NREQ
    my_lengths = lax.dynamic_slice_in_dim(lengths, first_req, NREQ, 0)
    my_steps = lax.dynamic_slice_in_dim(timesteps, first_req, NREQ, 0)
    stats = stats.reshape(NREQ, GROUP, BLK)
    norm_values = jnp.sqrt(jnp.sum(stats[:, :, 0], axis=1) / (my_lengths.astype(f32) * D))
    top = stats[:, :, 1:3].reshape(NREQ, HEADS)

    eps_cond, eps_uncond = pred[:NREQ, :, :16], pred[NREQ:, :, :16]
    guided = eps_uncond + guide_scale * (eps_cond - eps_uncond)
    varpart = pred[:NREQ, :, 16:]

    def own_channels(values):
        return lax.dynamic_slice_in_dim(values, copy_index * 8, 8, 2)

    slot_pos = lax.axis_index("seq") * SLOT + jnp.arange(SLOT, dtype=jnp.int32)
    query_ok = slot_pos[None, :] < my_lengths[:, None]
    guided_update = sampler_step(
        own_channels(patches),
        own_channels(noise),
        own_channels(guided),
        own_channels(varpart),
        my_steps.astype(f32)[:, None, None],
        query_ok[:, :, None],
    )
    return (guided_update, norm_values[None, :], top[None, :, :])


def solution(mesh):
    in_specs = (
        P("req", "seq", None),
        P("req", "seq", None),
        P(), P(), P(), P(), P(), P(), P(),
        P(None, ("req", "seq")),
        P("req", None),
        P(None, "req"),
        P(),
    )
    out_specs = (P("req", "seq", "cfg"), P("cfg", "req"), P("cfg", "req", None))
    return jax.shard_map(body, mesh=mesh, in_specs=in_specs, out_specs=out_specs, check_vma=False)
```

time: 771 us -> 80.1 us (0.10)
  the two profiles are of different devices: /device:TPU:2 before, /device:TPU:1 now
where the time goes in v1:
time: 80.1 us; the launch traced here: 78.8 us
  Pallas kernels  63.7 us (80%)
  local copies, waits for them, and re-layouts  6.85 us (9%)
  matrix products  4.04 us (5%)
  other arithmetic  3.45 us (4%)
    pallas_call x1, Pallas kernels, body(): pl.pallas_call(kernel, out_shape=(jax.ShapeDtypeStruct((8, SLOT, 32), f32...  63.7 us
    unnamed x23, local copies, waits for them, and re-layouts  4.44 us
    dot_general x1, matrix products, body(): mod_part = jnp.dot(cond_act, mod_w, preferred_element_type=jnp.float32)  2.32 us
    dot_general x1, matrix products, body(): jnp.dot(time_hidden, time_w2, preferred_element_type=jnp.float32)  1.72 us

profile of v1, /device:TPU:1, one launch (start us, length us, event | category | flops | bytes accessed | tf_op | source)
XLA Modules:
  0.0 78.8 jit_solution(17016500432040521500)
XLA Ops:
  0.6 0.0 copy-start
  0.7 0.9 %fusion.28 = (f32[4]{0:T(128)S(1)}, f32[4]{0:T(128)S(1)}) fusion(s32[16]{0:T(128)} %param.19, s32[]{:T(128)S(6)} %select_n.22), kind=kLoop, calls=%fused_computation.44 | loop fusion | flops 24 | bytes 52 | tf_op jit(solution)/shard_map/sqrt | solution.py:67
  1.6 0.7 convert_element_type.20
  2.3 0.1 fusion.11
  2.4 0.0 copy-done
  2.4 0.0 copy-start.4
  2.4 0.0 copy-start.1
  2.4 1.7 %fusion.6 = f32[16,1152]{1,0:T(8,128)S(1)} fusion(bf16[1152,1152]{1,0:T(8,128)(2,1)S(1)} %copy-done, bf16[256,1152]{1,0:T(8,128)(2,1)} %param.22, bf16[16,128]{1,0:T(8,128)(2,1)S(1)} %get-tuple-element.26, bf16[16,128]{1,0:T(8,128)(2,1)S(1)} %get-tuple-element.25), kind=kOutput, calls=%fused_computation.12 | convolution fusion | flops 52013056 | bytes 3325952 | tf_op jit(solution)/shard_map/dot_general | solution.py:345
  4.2 0.0 copy-start.3
  4.2 2.3 %fusion = f32[16,45]{1,0:T(8,128)S(1)} fusion(bf16[1152,45]{0,1:T(8,128)(2,1)} %param.26, f32[16,1152]{1,0:T(8,128)S(1)} %fusion.6, bf16[1001,1152]{1,0:T(8,128)(2,1)} %param.24, s32[16]{0:T(128)S(1)} %broadcast_select_fusion), kind=kOutput, calls=%fused_computation.2 | convolution fusion | flops 38686352 | bytes 2486656 | tf_op jit(solution)/shard_map/dot_general | solution.py:351
  6.5 0.6 pad.4
  7.1 0.0 copy-done.4
  7.1 0.7 copy.28.patches_ref
  7.8 0.0 copy-done.1
  7.8 1.2 %copy.30.outw_hbm = bf16[1152,288]{1,0:T(8,128)(2,1)} copy(bf16[1152,288]{0,1:T(8,128)(2,1)S(1)} %copy-done.1) | data formatting | bytes 1327104 | tf_op args[11]
  9.1 0.0 copy-done.3
  9.1 0.0 copy-start.6
  9.1 0.0 copy-start.7
  9.1 0.0 copy-start.5
  9.1 0.0 copy-start.2
  9.1 0.9 %copy.31.headw_ref = bf16[1152,32]{1,0:T(8,128)(2,1)} copy(bf16[1152,32]{0,1:T(8,128)(2,1)S(1)} %copy-done.3) | data formatting | bytes 147456 | tf_op args[12]
  10.0 63.7 %guided_block.1 = (f32[8,32,32]{2,1,0:T(8,128)}, f32[32,1,128]{2,1,0:T(1,128)}) custom-call(s32[16]{0:T(128)} %len_ref.1, f32[4,32,16]{2,1,0:T(8,128)} %copy.28.patches_ref, f32[16,1,128]{2,1,0:T(1,128)} %bitcast.11, bf16[288,3456]{1,0:T(8,128)(2,1)} %qkv_hbm.1, bf16[1152,288]{1,0:T(8,128)(2,1)} %copy.30.outw_hbm, bf16[1152,32]{1,0:T(8,128)(2,1)} %copy.31.headw_ref, ...), custom_call_target="tpu_custom_call" | custom-call | tf_op jit(solution)/shard_map/guided_block/pallas_call | solution.py:358
  73.7 0.8 %slice_reduce_fusion = f32[4]{0:T(128)S(1)} fusion(f32[4,8,128]{2,1,0:T(8,128)} %bitcast.9), kind=kLoop, calls=%fused_computation.16 | loop fusion | flops 28 | bytes 144 | tf_op jit(solution)/shard_map/reduce_sum | solution.py:399
  74.5 0.0 copy-done.6
  74.5 0.0 copy-done.7
  74.6 0.6 sqrt_bitcast_fusion
  75.2 0.1 broadcast_compare_fusion
  75.3 0.0 copy-done.5
  75.3 0.1 copy.37
  75.4 1.0 %fusion.29 = (f32[4,32,16]{2,1,0:T(8,128)S(1)}, f32[4,32,16]{2,1,0:T(8,128)S(1)}, f32[4,32,16]{2,1,0:T(8,128)S(1)}) fusion(f32[8,32,32]{2,1,0:T(8,128)} %get-tuple-element.5), kind=kLoop, calls=%fused_computation.45 | loop fusion | bytes 49152 | tf_op jit(solution)/shard_map/slice | solution.py:402
  76.4 0.0 copy-done.2
  76.4 0.2 add_select_fusion
  76.6 0.7 copy.35
  77.2 0.8 %slice.21 = f32[4,8,2]{2,1,0:T(8,128)S(1)} slice(f32[4,8,128]{2,1,0:T(8,128)} %bitcast.10), slice={[0:4], [0:8], [1:3]} | slice | bytes 512 | tf_op jit(solution)/shard_map/slice | solution.py:400
  78.0 0.1 copy.38
  78.2 0.7 copy.36
  (5 shorter events, 0.0 us)
Async XLA Ops:
  0.6 1.8 %copy-start = (bf16[1152,1152]{1,0:T(8,128)(2,1)S(1)}, bf16[1152,1152]{1,0:T(8,128)(2,1)}, u32[]{:S(2)}) copy-start(bf16[1152,1152]{1,0:T(8,128)(2,1)} %param.23) | copy-start | bytes 7962628
  2.4 4.7 %copy-start.4 = (f32[4,32,16]{1,2,0:T(8,128)S(1)}, f32[4,32,16]{1,2,0:T(8,128)}, u32[]{:S(2)}) copy-start(f32[4,32,16]{1,2,0:T(8,128)} %param.17) | copy-start | bytes 24580
  2.4 5.4 %copy-start.1 = (bf16[1152,288]{0,1:T(8,128)(2,1)S(1)}, bf16[1152,288]{0,1:T(8,128)(2,1)}, u32[]{:S(2)}) copy-start(bf16[1152,288]{0,1:T(8,128)(2,1)} %param.28) | copy-start | bytes 1990660
  4.2 4.9 %copy-start.3 = (bf16[1152,32]{0,1:T(8,128)(2,1)S(1)}, bf16[1152,32]{0,1:T(8,128)(2,1)}, u32[]{:S(2)}) copy-start(bf16[1152,32]{0,1:T(8,128)(2,1)} %param.29) | copy-start | bytes 221188
  9.1 65.5 %copy-start.6 = (s32[16]{0:T(128)S(1)}, s32[16]{0:T(128)}, u32[]{:S(2)}) copy-start(s32[16]{0:T(128)} %len_ref.1) | copy-start | bytes 196
  9.1 65.5 %copy-start.7 = (s32[16]{0:T(128)S(1)}, s32[16]{0:T(128)}, u32[]{:S(2)}) copy-start(s32[16]{0:T(128)} %param.19) | copy-start | bytes 196
  9.1 66.2 %copy-start.5 = (f32[4,32,16]{1,2,0:T(8,128)S(1)}, f32[4,32,16]{1,2,0:T(8,128)}, u32[]{:S(2)}) copy-start(f32[4,32,16]{1,2,0:T(8,128)} %param.18) | copy-start | bytes 24580
  9.1 67.3 %copy-start.2 = (f32[4,32,16]{2,1,0:T(8,128)S(1)}, f32[4,32,16]{2,1,0:T(8,128)}, u32[]{:S(2)}) copy-start(f32[4,32,16]{2,1,0:T(8,128)} %copy.28.patches_ref) | copy-start | bytes 24580

commit v2 on v1

v2 whole, which is shorter than its diff:
```python
import math

import jax
import jax.numpy as jnp
import numpy as np
from jax import lax
from jax.experimental import pallas as pl
from jax.experimental.pallas import tpu as pltpu
from jax.sharding import PartitionSpec as P

HEADS = 16
FREQ = 256
D = 1152
SEQ_TOTAL = 1024
NSEQ = 32
NREQ = 4
NDEV = NSEQ * NREQ
GROUP = 8
SLOT = 32
BLK = 128
WIN = 256
PAIR = 144
HEAD_DIM = 72
ROWS = 288
HALF = 144
MODC = 45
MESH = pl.DeviceIdType.MESH

norm_eps = 1e-06
masked_score = -1e30
guide_scale = 4.0
plan_offset = 0.008
diffusion_steps = 1000.0
INV_ROOT = 1.0 / math.sqrt(HEAD_DIM)
EXP_SCALE = INV_ROOT * math.log2(math.e)


def position_factors():
    half = D // 2
    rates = np.exp(-math.log(10000.0) * np.arange(half) / half)
    coarse = (SLOT * np.arange(NSEQ))[:, None] * rates[None, :]
    fine = np.arange(SLOT)[:, None] * rates[None, :]
    sc, cc, sf, cf = np.sin(coarse), np.cos(coarse), np.sin(fine), np.cos(fine)
    p1 = np.concatenate([sc, cc], axis=1)[:, None, :]
    p2 = np.concatenate([cc, -sc], axis=1)[:, None, :]
    q1 = np.concatenate([cf, cf], axis=1)
    q2 = np.concatenate([sf, sf], axis=1)
    return [jnp.asarray(t.astype(np.float32)) for t in (p1, p2, q1, q2)]


def alpha_bar(steps):
    phase = (steps / diffusion_steps + plan_offset) / (1.0 + plan_offset) * (math.pi / 2.0)
    return jnp.cos(phase) ** 2


def sampler_plan(patches, noise, steps, valid):
    abar = alpha_bar(steps)
    abar_prev = alpha_bar(steps - 1.0)
    beta = 1.0 - abar / abar_prev
    tilde = beta * (1.0 - abar_prev) / (1.0 - abar)
    root_rest, root, log_beta, log_tilde = jnp.sqrt(1.0 - abar), jnp.sqrt(abar), jnp.log(beta), jnp.log(tilde)
    on_start = beta * jnp.sqrt(abar_prev) / (1.0 - abar)
    from_patches = (1.0 - abar_prev) * jnp.sqrt(1.0 - beta) / (1.0 - abar) * patches

    def finish(guided, varpart):
        mean = on_start * ((patches - root_rest * guided) / root) + from_patches
        frac = (varpart + 1.0) * 0.5
        logvar = frac * log_beta + (1.0 - frac) * log_tilde
        return jnp.where(valid, mean + jnp.exp(0.5 * logvar) * noise, 0.0)

    return finish


def layer_norm(values):
    center = values - jnp.mean(values, axis=-1, keepdims=True)
    spread = jnp.mean(center * center, axis=-1, keepdims=True)
    return center * lax.rsqrt(spread + norm_eps)


def silu(values):
    return values / (1.0 + jnp.exp(-values))


NT = (((1,), (1,)), ((), ()))


def kernel(
    len_ref, step_ref, label_ref,
    patches_ref, noise_ref, w1_hbm, w2_hbm, table_hbm, modw_hbm, rates_ref, qkv_hbm, outw_hbm, headw_ref, patchw_ref,
    p1_ref, p2_ref, q1_ref, q2_ref,
    guided_out, norm_out, top_out,
    w1, w2, table, modw, modp,
    pb, patch_all, mod_all, mod_rows, xhat, hid0, wbuf, outbuf, qbuf, kbuf, vbuf, mbuf, mixin, predsend, pred_in,
    stat_send, stat_in, top,
    ld, mod_s, mod_r, pat_s, pat_r, w_s, w_r, wl, wf_s, wf_r, o_s, o_r, ol, of_s, of_r, mx_s, mx_r, pr_s, pr_r, st_s, st_r,
):
    g = lax.axis_index("cfg")
    y = lax.axis_index("req")
    s = lax.axis_index("seq")
    other = 1 - g
    me = y * NSEQ + s
    q = lax.div(s, GROUP)
    j = lax.rem(s, GROUP)

    def remote(src, dst, ssem, rsem, dev):
        return pltpu.make_async_remote_copy(
            src_ref=src, dst_ref=dst, send_sem=ssem, recv_sem=rsem, device_id=dev, device_id_type=MESH
        )

    def wait_bytes(ref, sem):
        pltpu.make_async_copy(ref, ref, sem).wait()

    def each_other(act):
        reqs = [lax.rem(y + dy, NREQ) for dy in range(NREQ)]
        for dy in range(1, NREQ):
            act(reqs[dy], s)

        def step(k, _):
            ts = lax.rem(s + k, NSEQ)
            for ty in reqs:
                act(ty, ts)
            return 0

        lax.fori_loop(1, NSEQ, step, 0)

    bar = pltpu.get_barrier_semaphore()
    each_other(lambda ty, ts: pl.semaphore_signal(bar, inc=1, device_id=(g, ty, ts), device_id_type=MESH))
    for qq in range(NREQ):
        pl.semaphore_signal(bar, inc=1, device_id=(other, y, qq * GROUP + lax.div(s, NREQ)), device_id_type=MESH)
    pl.semaphore_signal(bar, inc=1, device_id=(other, y, s), device_id_type=MESH)

    loads = []
    for i, (src, dst) in enumerate(((w1_hbm, w1), (w2_hbm, w2), (table_hbm, table), (modw_hbm, modw))):
        c = pltpu.make_async_copy(src, dst, ld.at[i])
        c.start()
        loads.append(c)
    col = pl.multiple_of(j * BLK, BLK)
    local_w = []
    for kind in range(3):
        c = pltpu.make_async_copy(
            qkv_hbm.at[:, pl.ds(pl.multiple_of(kind * D + col, BLK), WIN)],
            wbuf.at[kind, pl.ds(pl.multiple_of(ROWS * y, 16), ROWS), :],
            wl.at[kind],
        )
        c.start()
        local_w.append(c)
    local_o = pltpu.make_async_copy(outw_hbm, outbuf.at[pl.ds(pl.multiple_of(ROWS * y, 16), ROWS), :], ol)
    local_o.start()

    for r in range(NREQ):
        pb[r] = jnp.transpose(patches_ref[r]).astype(jnp.bfloat16)

    req_row = lax.broadcasted_iota(jnp.int32, (16, 1), 0)
    times = jnp.zeros((16, 1), jnp.int32)
    used = jnp.zeros((16, 1), jnp.int32)
    for r in range(16):
        times = jnp.where(req_row == r, step_ref[r], times)
        used = jnp.where(req_row == r, label_ref[r], used)
    used = jnp.where(g == 0, used, 1000)
    angles = times.astype(jnp.float32) * rates_ref[...]
    tfreq = jnp.concatenate([jnp.cos(angles), jnp.sin(angles)], axis=1).astype(jnp.bfloat16)
    one_hot = jnp.where(lax.broadcasted_iota(jnp.int32, (16, 1001), 1) == used, 1.0, 0.0).astype(jnp.bfloat16)
    loads[0].wait()
    time_hidden = silu(jnp.dot(tfreq, w1[...], preferred_element_type=jnp.float32)).astype(jnp.bfloat16)
    loads[1].wait()
    cond = jnp.dot(time_hidden, w2[...], preferred_element_type=jnp.float32)
    loads[2].wait()
    cond = cond + jnp.dot(one_hot, table[...], preferred_element_type=jnp.float32)
    cond_act = silu(cond).astype(jnp.bfloat16)
    loads[3].wait()
    mod_part = lax.dot_general(cond_act, modw[...], NT, preferred_element_type=jnp.float32)
    modp[...] = jnp.zeros_like(modp)
    for r in range(16):
        modp[r, :, :MODC] = mod_part[r : r + 1, :]

    pl.semaphore_wait(bar, NDEV - 1 + NREQ + 1)

    def send_patch(k, _):
        d = lax.rem(s + k, NSEQ)
        remote(pb.at[lax.div(d, GROUP)], patch_all.at[s], pat_s, pat_r, (g, y, d)).start()
        return 0

    lax.fori_loop(1, NSEQ, send_patch, 0)

    each_other(
        lambda ty, ts: remote(
            modp.at[ty * NREQ + lax.div(ts, GROUP)], mod_all.at[me], mod_s, mod_r, (g, ty, ts)
        ).start()
    )

    up, down = lax.rem(y + 1, NREQ), lax.rem(y + 3, NREQ)
    onward = lax.rem(y + 1 + 2 * g, NREQ)
    behind = lax.rem(y + 3 + 2 * g, NREQ)
    across = lax.rem(y + 2, NREQ)

    def w_part(ry, core):
        return wbuf.at[:, pl.ds(pl.multiple_of(ROWS * ry + HALF * core, 16), HALF), :]

    def o_part(ry, core):
        return outbuf.at[pl.ds(pl.multiple_of(ROWS * ry + HALF * core, 16), HALF), :]

    for i, ty in enumerate((up, down)):
        for kind in range(3):
            remote(
                qkv_hbm.at[pl.ds(pl.multiple_of(HALF * g, 16), HALF), pl.ds(pl.multiple_of(kind * D + col, BLK), WIN)],
                wbuf.at[kind, pl.ds(pl.multiple_of(ROWS * y + HALF * g, 16), HALF), :],
                w_s.at[i],
                w_r.at[i],
                (g, ty, s),
            ).start()

    mod_all[me] = modp[y * NREQ + q]
    patch_all[s] = pb[q]
    length = len_ref[y * NREQ + q]
    wait_bytes(patch_all.at[pl.ds(0, NSEQ - 1)], pat_r)

    def embed(first_source, count):
        x = patch_all[pl.ds(first_source, count)].reshape(count * SLOT, 16)
        h = jnp.dot(x, patchw_ref[...], preferred_element_type=jnp.float32)
        places = [
            p1_ref[first_source + i] * q1_ref[...] + p2_ref[first_source + i] * q2_ref[...] for i in range(count)
        ]
        return h + jnp.concatenate(places, axis=0)

    def normalise(b, _):
        xhat[pl.ds(pl.multiple_of(b * BLK, BLK), BLK), :] = layer_norm(embed(b * 4, 4))
        return 0

    lax.fori_loop(0, GROUP, normalise, 0)

    wait_bytes(w_part(0, 0), w_r.at[g])
    w_relay = remote(w_part(behind, g), w_part(behind, g), w_s.at[2], w_r.at[2], (g, onward, s))
    w_relay.start()
    w_forwards = [remote(w_part(behind, g), w_part(behind, g), wf_s.at[0], wf_r.at[0], (other, y, s))]
    w_forwards[0].start()
    o_own = o_part(y, g)
    o_mine = outw_hbm.at[pl.ds(pl.multiple_of(HALF * g, 16), HALF), :]
    o_copies = [remote(o_mine, o_own, o_s.at[i], o_r.at[i], (g, ty, s)) for i, ty in enumerate((up, down))]
    for c in o_copies:
        c.start()
    wait_bytes(w_part(0, 0), w_r.at[other])
    w_forwards.append(remote(w_part(onward, g), w_part(onward, g), wf_s.at[1], wf_r.at[1], (other, y, s)))
    w_forwards[1].start()

    wait_bytes(mod_all.at[pl.ds(0, NDEV - 1)], mod_r)
    lane_row = lax.broadcasted_iota(jnp.int32, (1, BLK), 1)
    for tile in range(5 * D // BLK):
        first = (tile * BLK) // MODC
        last = (tile * BLK + BLK - 1) // MODC
        value = None
        for source in range(first, last + 1):
            at = source * MODC - tile * BLK
            piece = mod_all[source]
            if at % BLK:
                piece = pltpu.roll(piece, at % BLK, 1)
            value = piece if value is None else jnp.where(lane_row >= at, piece, value)
        mod_rows[tile // 9, :, (tile % 9) * BLK : (tile % 9 + 1) * BLK] = value
    hid0[...] = embed(j * 4, 4)

    w_relay.wait_recv()
    w_forwards.append(remote(w_part(across, g), w_part(across, g), wf_s.at[2], wf_r.at[2], (other, y, s)))
    w_forwards[2].start()
    for c in local_w:
        c.wait()
    for f in w_forwards:
        f.wait_recv()

    lane = lax.broadcasted_iota(jnp.int32, (1, WIN), 1)
    low = j * 16
    in_a = (lane >= low) & (lane < low + HEAD_DIM)
    in_b = (lane >= low + HEAD_DIM) & (lane < low + PAIR)
    spare = lane == lax.rem(low + PAIR, WIN)

    def project(b, _):
        rows = pl.ds(pl.multiple_of(b * 256, 256), 256)
        normed = (xhat[rows, :] * (1.0 + mod_rows[1]) + mod_rows[0]).astype(jnp.bfloat16)
        qbuf[rows, :] = jnp.dot(normed, wbuf[0], preferred_element_type=jnp.float32).astype(jnp.bfloat16)
        keys = jnp.dot(normed, wbuf[1], preferred_element_type=jnp.float32)
        place = b * 256 + lax.broadcasted_iota(jnp.int32, (256, 1), 0)
        bias = jnp.where(place < length, 0.0, masked_score)
        kbuf[rows, :] = jnp.where(spare, bias, keys).astype(jnp.bfloat16)
        vbuf[rows, :] = jnp.dot(normed, wbuf[2], preferred_element_type=jnp.float32).astype(jnp.bfloat16)
        return 0

    lax.fori_loop(0, 4, project, 0)

    wait_bytes(o_part(0, 0), o_r.at[g])
    o_relay = remote(o_part(behind, g), o_part(behind, g), o_s.at[2], o_r.at[2], (g, onward, s))
    o_relay.start()
    o_forwards = [remote(o_part(behind, g), o_part(behind, g), of_s.at[0], of_r.at[0], (other, y, s))]
    o_forwards[0].start()
    wait_bytes(o_part(0, 0), o_r.at[other])
    o_forwards.append(remote(o_part(onward, g), o_part(onward, g), of_s.at[1], of_r.at[1], (other, y, s)))
    o_forwards[1].start()
    o_forwards.append(remote(o_part(across, g), o_part(across, g), of_s.at[2], of_r.at[2], (other, y, s)))

    top[...] = jnp.full_like(top, masked_score)

    def attend(k, _):
        b = lax.rem(j + k, GROUP)
        rows = pl.ds(pl.multiple_of(b * BLK, BLK), BLK)
        query = qbuf[rows, :].astype(jnp.float32)
        live = b * BLK + lax.broadcasted_iota(jnp.int32, (BLK, 1), 0) < length
        mixed = jnp.zeros((BLK, WIN), jnp.float32)
        for head, inside in enumerate((in_a, in_b)):
            mine = jnp.where(inside, query, jnp.where(spare, 1.0, 0.0)).astype(jnp.bfloat16)
            raw = lax.dot_general(mine, kbuf[...], NT, preferred_element_type=jnp.float32)
            peak = jnp.max(raw, axis=1, keepdims=True)
            expo = jnp.exp2((raw - peak) * EXP_SCALE)
            total = jnp.sum(expo, axis=1, keepdims=True)
            summed = jnp.dot(expo.astype(jnp.bfloat16), vbuf[...], preferred_element_type=jnp.float32)
            mixed = jnp.where(inside, summed * (1.0 / total), mixed)
            best = jnp.max(jnp.where(live, peak, masked_score), axis=0, keepdims=True)
            top[head] = jnp.maximum(top[head], best)
        mbuf[b] = mixed.astype(jnp.bfloat16)

        @pl.when(k < GROUP)
        def _():
            remote(mbuf.at[b], mixin.at[j], mx_s, mx_r, (g, y, q * GROUP + b)).start()

        @pl.when(k == GROUP - 2)
        def _():
            o_relay.wait_recv()
            o_forwards[2].start()

        return 0

    lax.fori_loop(1, GROUP + 1, attend, 0)
    mixin[j] = mbuf[j]
    local_o.wait()
    for f in o_forwards:
        f.wait_recv()
    wait_bytes(mixin.at[pl.ds(0, GROUP - 1)], mx_r)

    tiles = []
    for t in range(9):
        tile = mixin[t, :, :BLK] if t < GROUP else None
        if t > 0:
            rest = mixin[t - 1, :, BLK:]
            tile = rest if tile is None else tile + rest
        tiles.append(tile)
    mixed_all = jnp.concatenate(tiles, axis=1)
    attended = lax.dot_general(mixed_all, outbuf[...], NT, preferred_element_type=jnp.float32)
    hidden1 = hid0[...] + mod_rows[2] * attended
    place = j * BLK + lax.broadcasted_iota(jnp.int32, (BLK, 1), 0)
    squares = jnp.sum(
        jnp.sum(jnp.where(place < length, hidden1 * hidden1, 0.0), axis=1, keepdims=True), axis=0, keepdims=True
    )
    stat = jnp.where(
        lane_row == 2 * j,
        top[0] * INV_ROOT,
        jnp.where(lane_row == 2 * j + 1, top[1] * INV_ROOT, jnp.where(lane_row == HEADS, squares, 0.0)),
    )
    stat_send[...] = stat

    def send_stat(k, _):
        d = lax.rem(s + k, NSEQ)
        remote(stat_send, stat_in.at[s], st_s, st_r, (g, y, d)).start()
        return 0

    lax.fori_loop(1, NSEQ, send_stat, 0)
    stat_in[s] = stat

    normed2 = (layer_norm(hidden1) * (1.0 + mod_rows[4]) + mod_rows[3]).astype(jnp.bfloat16)
    prediction = lax.dot_general(headw_ref[...], normed2, NT, preferred_element_type=jnp.float32)
    slot = g * NREQ + q
    p_copies = []
    for i in range(NREQ):
        for gg in range(2):
            for part in range(2):
                predsend[gg * NREQ + i, 8 * part : 8 * part + 8, :] = prediction[
                    16 * part + 8 * gg : 16 * part + 8 * gg + 8, SLOT * i : SLOT * i + SLOT
                ]
            ts = j * NREQ + i
            self_copy = (ts == s) & (g == gg)
            c = remote(predsend.at[gg * NREQ + i], pred_in.at[slot], pr_s.at[i * 2 + gg], pr_r, (gg, y, ts))
            p_copies.append((self_copy, c))

            @pl.when(jnp.logical_not(self_copy))
            def _():
                c.start()

            @pl.when(self_copy)
            def _():
                pltpu.make_async_copy(predsend.at[gg * NREQ + i], pred_in.at[slot], pr_r).start()

    shape = (NREQ, 8, SLOT)
    which = lax.broadcasted_iota(jnp.int32, shape, 0)
    steps = jnp.zeros(shape, jnp.int32)
    limits = jnp.zeros(shape, jnp.int32)
    for r in range(NREQ):
        steps = jnp.where(which == r, step_ref[y * NREQ + r], steps)
        limits = jnp.where(which == r, len_ref[y * NREQ + r], limits)
    valid = s * SLOT + lax.broadcasted_iota(jnp.int32, shape, 2) < limits
    channels = pl.ds(pl.multiple_of(g * 8, 8), 8)
    own_patches = patches_ref[:, channels, :]
    own_noise = noise_ref[:, channels, :]
    finish = sampler_plan(own_patches, own_noise, steps.astype(jnp.float32), valid)

    wait_bytes(pred_in, pr_r)
    eps_cond, eps_uncond = pred_in[:NREQ, :8, :], pred_in[NREQ:, :8, :]
    guided = eps_uncond + guide_scale * (eps_cond - eps_uncond)
    guided_out[...] = finish(guided, pred_in[:NREQ, 8:, :])

    wait_bytes(stat_in.at[pl.ds(0, NSEQ - 1)], st_r)
    for r in range(NREQ):
        row = stat_in[r * GROUP]
        for i in range(1, GROUP):
            row = row + stat_in[r * GROUP + i]
        top_out[r : r + 1, :] = row[:, :HEADS]
        count = jnp.full((1, 1), len_ref[y * NREQ + r], jnp.int32).astype(jnp.float32) * D
        norm_out[:, r : r + 1] = jnp.sqrt(row[:, HEADS : HEADS + 1] / count)

    wait_bytes(mod_all.at[pl.ds(0, NDEV - 1)], mod_s)
    wait_bytes(patch_all.at[pl.ds(0, NSEQ - 1)], pat_s)
    wait_bytes(mixin.at[pl.ds(0, GROUP - 1)], mx_s)
    wait_bytes(stat_in.at[pl.ds(0, NSEQ - 1)], st_s)
    for i in range(2):
        wait_bytes(w_part(0, 0), w_s.at[i])
    for c in [w_relay, o_relay] + w_forwards + o_copies + o_forwards:
        c.wait_send()
    for self_copy, c in p_copies:

        @pl.when(jnp.logical_not(self_copy))
        def _():
            c.wait_send()


def body(
    patches, noise, timesteps, labels, lengths, time_w1, time_w2, label_table, patch_w, mod_w, qkv_w, out_w, head_w
):
    vmem = pl.BlockSpec(memory_space=pltpu.VMEM)
    hbm = pl.BlockSpec(memory_space=pl.ANY)
    smem = pl.BlockSpec(memory_space=pltpu.SMEM)
    bf, f32 = jnp.bfloat16, jnp.float32
    dma = pltpu.SemaphoreType.DMA
    rates = np.exp(-math.log(10000.0) * np.arange(FREQ // 2) / (FREQ // 2)).astype(np.float32)[None, :]
    guided, norms, top = pl.pallas_call(
        kernel,
        out_shape=(
            jax.ShapeDtypeStruct((NREQ, 8, SLOT), f32),
            jax.ShapeDtypeStruct((1, NREQ), f32),
            jax.ShapeDtypeStruct((NREQ, HEADS), f32),
        ),
        in_specs=[smem] * 3 + [vmem] * 2 + [hbm] * 4 + [vmem] + [hbm] * 2 + [vmem] * 6,
        out_specs=(vmem, vmem, vmem),
        scratch_shapes=[
            pltpu.VMEM((FREQ, D), bf),
            pltpu.VMEM((D, D), bf),
            pltpu.VMEM((1001, D), bf),
            pltpu.VMEM((MODC, D), bf),
            pltpu.VMEM((16, 1, BLK), f32),
            pltpu.VMEM((4, SLOT, 16), bf),
            pltpu.VMEM((NSEQ, SLOT, 16), bf),
            pltpu.VMEM((NDEV, 1, BLK), f32),
            pltpu.VMEM((5, 1, D), f32),
            pltpu.VMEM((SEQ_TOTAL, D), f32),
            pltpu.VMEM((BLK, D), f32),
            pltpu.VMEM((3, D, WIN), bf),
            pltpu.VMEM((D, D), bf),
            pltpu.VMEM((SEQ_TOTAL, WIN), bf),
            pltpu.VMEM((SEQ_TOTAL, WIN), bf),
            pltpu.VMEM((SEQ_TOTAL, WIN), bf),
            pltpu.VMEM((GROUP, BLK, WIN), bf),
            pltpu.VMEM((GROUP, BLK, WIN), bf),
            pltpu.VMEM((8, 16, SLOT), f32),
            pltpu.VMEM((8, 16, SLOT), f32),
            pltpu.VMEM((1, BLK), f32),
            pltpu.VMEM((NSEQ, 1, BLK), f32),
            pltpu.VMEM((2, 1, 1), f32),
            dma((4,)), dma, dma, dma, dma,
            dma((3,)), dma((3,)), dma((3,)), dma((3,)), dma((3,)),
            dma((3,)), dma((3,)), dma, dma((3,)), dma((3,)),
            dma, dma, dma((8,)), dma, dma, dma,
        ],
        compiler_params=pltpu.CompilerParams(
            collective_id=0, has_side_effects=True, vmem_limit_bytes=56 * 1024 * 1024
        ),
        name="guided_block",
    )(
        lengths, timesteps, labels,
        jnp.transpose(patches, (0, 2, 1)), jnp.transpose(noise, (0, 2, 1)),
        time_w1, time_w2, label_table, jnp.transpose(mod_w), jnp.asarray(rates), qkv_w, jnp.transpose(out_w),
        jnp.transpose(head_w), patch_w, *position_factors(),
    )
    return (jnp.transpose(guided, (0, 2, 1)), norms, top[None, :, :])


def solution(mesh):
    in_specs = (
        P("req", "seq", None),
        P("req", "seq", None),
        P(), P(), P(), P(), P(), P(), P(),
        P(None, ("req", "seq")),
        P("req", None),
        P(None, "req"),
        P(),
    )
    out_specs = (P("req", "seq", "cfg"), P("cfg", "req"), P("cfg", "req", None))
    return jax.shard_map(body, mesh=mesh, in_specs=in_specs, out_specs=out_specs, check_vma=False)
```

time: 80.1 us -> 63.7 us (0.80); the launches traced: 78.8 us -> 63.5 us
  Pallas kernels: 63.7 us -> 59.1 us
  matrix products: 4.04 us -> 0 us
  other arithmetic: 3.45 us -> 0 us
  local copies, waits for them, and re-layouts: 6.85 us -> 3.73 us
    pallas_call x1, Pallas kernels: 63.7 us -> 59.1 us  [body(): pl.pallas_call(kernel, out_shape=(jax.ShapeDtypeStruct((NREQ, 8, SLOT), f...]
    dot_general x2 -> x0, matrix products: 4.04 us -> none  [the longest x1 2.32 us: body(): mod_part = jnp.dot(cond_act, mod_w, preferred_element_type=jnp.float32)]
    slice x2 -> x0, local copies, waits for them, and re-layouts: 1.79 us -> none  [the longest x1 1.01 us: body(): eps_cond, eps_uncond = (pred[:NREQ, :, :16], pred[NREQ:, :, :16])]
    sqrt x1 -> x0, other arithmetic: 0.93 us -> none  [sampler_step(): start = (patches - jnp.sqrt(1.0 - abar) * guided) / jnp.sqrt(abar)]
    reduce_sum x1 -> x0, other arithmetic: 0.83 us -> none  [body(): jnp.sum(stats[:, :, 0], axis=1) / (my_lengths.astype(f32) * D)]
    unnamed x23 -> x3, local copies, waits for them, and re-layouts: 4.44 us -> 3.73 us
where the time goes in v2:
time: 63.7 us; the launch traced here: 63.5 us
  Pallas kernels  59.1 us (93%)
  local copies, waits for them, and re-layouts  3.73 us (6%)
  between operations  0.64 us (1%)
    pallas_call x1, Pallas kernels, body(): pl.pallas_call(kernel, out_shape=(jax.ShapeDtypeStruct((NREQ, 8, SLOT), f...  59.1 us
    unnamed x3, local copies, waits for them, and re-layouts  3.73 us

profile of v2, /device:TPU:1, one launch (start us, length us, event | category | flops | bytes accessed | tf_op | source)
XLA Modules:
  0.0 63.5 jit_solution(11546639690613692204)
XLA Ops:
  0.6 59.1 %guided_block.1 = (f32[4,8,32]{2,1,0:T(8,128)}, f32[1,4]{1,0:T(1,128)}, f32[4,16]{1,0:T(4,128)}) custom-call(s32[16]{0:T(128)} %len_ref.1, s32[16]{0:T(128)} %step_ref.1, s32[16]{0:T(128)} %label_ref.1, f32[4,16,32]{2,1,0:T(8,128)} %bitcast.10, f32[4,16,32]{2,1,0:T(8,128)} %bitcast.11, bf16[256,1152]{1,0:T(8,128)(2,1)} %w1_hbm.1, bf16[1152,1152]{1,0:T(8,128)(2,1)} %w2_hbm.1, ...), custom_call_target="tpu_custom_call" | custom-call | tf_op jit(solution)/shard_map/guided_block/pallas_call | solution.py:438
  59.8 1.3 %copy.24 = f32[4,32,8]{1,2,0:T(8,128)} copy(f32[4,32,8]{1,2,0:T(8,128)} %bitcast.12) | data formatting | bytes 8192
  61.1 1.2 %copy.25 = f32[1,4]{1,0:T(1,128)} copy(f32[1,4]{1,0:T(1,128)} %get-tuple-element.13) | data formatting | bytes 32
  62.3 1.2 %copy.26 = f32[1,4,16]{2,1,0:T(4,128)} copy(f32[1,4,16]{2,1,0:T(4,128)} %bitcast.13) | data formatting | bytes 512

commit v3 on v2

--- a/solution.py
+++ b/solution.py
@@ -14,7 +14,8 @@
 SEQ_TOTAL = 1024
 NSEQ = 32
 NREQ = 4
-NDEV = NSEQ * NREQ
+NX = 4
+NZ = 8
 GROUP = 8
 SLOT = 32
 BLK = 128
@@ -53,22 +54,19 @@
     return jnp.cos(phase) ** 2
 
 
-def sampler_plan(patches, noise, steps, valid):
+def sampler_step(patches, noise, guided, varpart, steps, valid):
     abar = alpha_bar(steps)
     abar_prev = alpha_bar(steps - 1.0)
     beta = 1.0 - abar / abar_prev
+    start = (patches - jnp.sqrt(1.0 - abar) * guided) / jnp.sqrt(abar)
+    mean = (
+        beta * jnp.sqrt(abar_prev) / (1.0 - abar) * start
+        + (1.0 - abar_prev) * jnp.sqrt(1.0 - beta) / (1.0 - abar) * patches
+    )
     tilde = beta * (1.0 - abar_prev) / (1.0 - abar)
-    root_rest, root, log_beta, log_tilde = jnp.sqrt(1.0 - abar), jnp.sqrt(abar), jnp.log(beta), jnp.log(tilde)
-    on_start = beta * jnp.sqrt(abar_prev) / (1.0 - abar)
-    from_patches = (1.0 - abar_prev) * jnp.sqrt(1.0 - beta) / (1.0 - abar) * patches
-
-    def finish(guided, varpart):
-        mean = on_start * ((patches - root_rest * guided) / root) + from_patches
-        frac = (varpart + 1.0) * 0.5
-        logvar = frac * log_beta + (1.0 - frac) * log_tilde
-        return jnp.where(valid, mean + jnp.exp(0.5 * logvar) * noise, 0.0)
-
-    return finish
+    frac = (varpart + 1.0) * 0.5
+    logvar = frac * jnp.log(beta) + (1.0 - frac) * jnp.log(tilde)
+    return jnp.where(valid, mean + jnp.exp(0.5 * logvar) * noise, 0.0)
 
 
 def layer_norm(values):
@@ -86,19 +84,19 @@
 
 def kernel(
     len_ref, step_ref, label_ref,
-    patches_ref, noise_ref, w1_hbm, w2_hbm, table_hbm, modw_hbm, rates_ref, qkv_hbm, outw_hbm, headw_ref, patchw_ref,
+    patches_ref, w1_hbm, w2_hbm, table_hbm, modw_hbm, rates_ref, qkv_hbm, outw_hbm, headw_ref, patchw_ref,
     p1_ref, p2_ref, q1_ref, q2_ref,
-    guided_out, norm_out, top_out,
+    pred_out, stat_out,
     w1, w2, table, modw, modp,
-    pb, patch_all, mod_all, mod_rows, xhat, hid0, wbuf, outbuf, qbuf, kbuf, vbuf, mbuf, mixin, predsend, pred_in,
+    pb, patch_x, patch_m, patch_z, mod_y, mod_x, mod_z, mod_rows, xhat, hid0, wbuf, outbuf, qbuf, kbuf, vbuf, mbuf, mixin, predsend, pred_in,
     stat_send, stat_in, top,
-    ld, mod_s, mod_r, pat_s, pat_r, w_s, w_r, wl, wf_s, wf_r, o_s, o_r, ol, of_s, of_r, mx_s, mx_r, pr_s, pr_r, st_s, st_r,
+    ld, my_s, my_r, mx_s2, mx_r2, mz_s, mz_r, px_s, px_r, pz_s, pz_r, w_s, w_r, wl, wf_s, wf_r, o_s, o_r, ol, of_s, of_r, mx_s, mx_r, pr_s, pr_r, st_s, st_r,
 ):
     g = lax.axis_index("cfg")
     y = lax.axis_index("req")
     s = lax.axis_index("seq")
     other = 1 - g
-    me = y * NSEQ + s
+    z, x = lax.div(s, NX), lax.rem(s, NX)
     q = lax.div(s, GROUP)
     j = lax.rem(s, GROUP)
 
@@ -110,24 +108,15 @@
     def wait_bytes(ref, sem):
         pltpu.make_async_copy(ref, ref, sem).wait()
 
-    def each_other(act):
-        reqs = [lax.rem(y + dy, NREQ) for dy in range(NREQ)]
-        for dy in range(1, NREQ):
-            act(reqs[dy], s)
-
-        def step(k, _):
-            ts = lax.rem(s + k, NSEQ)
-            for ty in reqs:
-                act(ty, ts)
-            return 0
-
-        lax.fori_loop(1, NSEQ, step, 0)
-
     bar = pltpu.get_barrier_semaphore()
-    each_other(lambda ty, ts: pl.semaphore_signal(bar, inc=1, device_id=(g, ty, ts), device_id_type=MESH))
-    for qq in range(NREQ):
-        pl.semaphore_signal(bar, inc=1, device_id=(other, y, qq * GROUP + lax.div(s, NREQ)), device_id_type=MESH)
-    pl.semaphore_signal(bar, inc=1, device_id=(other, y, s), device_id_type=MESH)
+    in_block = 4 * z + NX - 8 * lax.rem(z, 2)
+    near = [(g, lax.rem(y + k, NREQ), s) for k in range(1, NREQ)]
+    near += [(g, y, z * NX + lax.rem(x + k, NX)) for k in range(1, NX)]
+    near += [(g, y, lax.rem(z + k, NZ) * NX + x) for k in range(1, NZ)]
+    near += [(g, y, in_block + lax.rem(x + k, NX)) for k in range(1, NX)]
+    near += [(other, y, s)]
+    for device in near:
+        pl.semaphore_signal(bar, inc=1, device_id=device, device_id_type=MESH)
 
     loads = []
     for i, (src, dst) in enumerate(((w1_hbm, w1), (w2_hbm, w2), (table_hbm, table), (modw_hbm, modw))):
@@ -147,8 +136,7 @@
     local_o = pltpu.make_async_copy(outw_hbm, outbuf.at[pl.ds(pl.multiple_of(ROWS * y, 16), ROWS), :], ol)
     local_o.start()
 
-    for r in range(NREQ):
-        pb[r] = jnp.transpose(patches_ref[r]).astype(jnp.bfloat16)
+    pb[...] = patches_ref[...].astype(jnp.bfloat16)
 
     req_row = lax.broadcasted_iota(jnp.int32, (16, 1), 0)
     times = jnp.zeros((16, 1), jnp.int32)
@@ -173,20 +161,13 @@
     for r in range(16):
         modp[r, :, :MODC] = mod_part[r : r + 1, :]
 
-    pl.semaphore_wait(bar, NDEV - 1 + NREQ + 1)
-
-    def send_patch(k, _):
-        d = lax.rem(s + k, NSEQ)
-        remote(pb.at[lax.div(d, GROUP)], patch_all.at[s], pat_s, pat_r, (g, y, d)).start()
-        return 0
-
-    lax.fori_loop(1, NSEQ, send_patch, 0)
-
-    each_other(
-        lambda ty, ts: remote(
-            modp.at[ty * NREQ + lax.div(ts, GROUP)], mod_all.at[me], mod_s, mod_r, (g, ty, ts)
-        ).start()
-    )
+    pl.semaphore_wait(bar, len(near))
+
+    for k in range(1, NREQ):
+        ty = lax.rem(y + k, NREQ)
+        remote(modp.at[pl.ds(ty * NREQ, NREQ)], mod_y.at[:, y], my_s, my_r, (g, ty, s)).start()
+    for k in range(1, NX):
+        remote(pb, patch_x.at[x], px_s, px_r, (g, y, z * NX + lax.rem(x + k, NX))).start()
 
     up, down = lax.rem(y + 1, NREQ), lax.rem(y + 3, NREQ)
     onward = lax.rem(y + 1 + 2 * g, NREQ)
@@ -209,24 +190,35 @@
                 (g, ty, s),
             ).start()
 
-    mod_all[me] = modp[y * NREQ + q]
-    patch_all[s] = pb[q]
+    mod_y[:, y] = modp[pl.ds(y * NREQ, NREQ)]
+    patch_x[x] = pb[...]
     length = len_ref[y * NREQ + q]
-    wait_bytes(patch_all.at[pl.ds(0, NSEQ - 1)], pat_r)
-
-    def embed(first_source, count):
-        x = patch_all[pl.ds(first_source, count)].reshape(count * SLOT, 16)
-        h = jnp.dot(x, patchw_ref[...], preferred_element_type=jnp.float32)
-        places = [
-            p1_ref[first_source + i] * q1_ref[...] + p2_ref[first_source + i] * q2_ref[...] for i in range(count)
-        ]
+
+    wait_bytes(mod_y.at[pl.ds(0, NREQ - 1)], my_r)
+    for k in range(1, NX):
+        remote(mod_y, mod_x.at[:, x], mx_s2, mx_r2, (g, y, z * NX + lax.rem(x + k, NX))).start()
+    mod_x[:, x] = mod_y[...]
+    wait_bytes(patch_x.at[pl.ds(0, NX - 1)], px_r)
+    for r in range(NREQ):
+        patch_m[r] = jnp.concatenate([patch_x[i, r] for i in range(NX)], axis=1)
+    for k in range(1, NZ):
+        tz = lax.rem(z + k, NZ)
+        remote(patch_m.at[lax.div(tz, 2)], patch_z.at[z], pz_s, pz_r, (g, y, tz * NX + x)).start()
+    patch_z[z] = patch_m[q]
+    wait_bytes(mod_x.at[pl.ds(0, NX - 1)], mx_r2)
+    for k in range(1, NZ):
+        tz = lax.rem(z + k, NZ)
+        remote(mod_x.at[lax.div(tz, 2)], mod_z.at[z], mz_s, mz_r, (g, y, tz * NX + x)).start()
+    mod_z[z] = mod_x[q]
+
+    def embed(b):
+        h = lax.dot_general(patch_z[b], patchw_ref[...], (((0,), (0,)), ((), ())), preferred_element_type=jnp.float32)
+        places = [p1_ref[b * 4 + i] * q1_ref[...] + p2_ref[b * 4 + i] * q2_ref[...] for i in range(4)]
         return h + jnp.concatenate(places, axis=0)
 
     def normalise(b, _):
-        xhat[pl.ds(pl.multiple_of(b * BLK, BLK), BLK), :] = layer_norm(embed(b * 4, 4))
+        xhat[pl.ds(pl.multiple_of(b * BLK, BLK), BLK), :] = layer_norm(embed(b))
         return 0
-
-    lax.fori_loop(0, GROUP, normalise, 0)
 
     wait_bytes(w_part(0, 0), w_r.at[g])
     w_relay = remote(w_part(behind, g), w_part(behind, g), w_s.at[2], w_r.at[2], (g, onward, s))
@@ -242,7 +234,10 @@
     w_forwards.append(remote(w_part(onward, g), w_part(onward, g), wf_s.at[1], wf_r.at[1], (other, y, s)))
     w_forwards[1].start()
 
-    wait_bytes(mod_all.at[pl.ds(0, NDEV - 1)], mod_r)
+    wait_bytes(patch_z.at[pl.ds(0, NZ - 1)], pz_r)
+    lax.fori_loop(0, GROUP, normalise, 0)
+
+    wait_bytes(mod_z.at[pl.ds(0, NZ - 1)], mz_r)
     lane_row = lax.broadcasted_iota(jnp.int32, (1, BLK), 1)
     for tile in range(5 * D // BLK):
         first = (tile * BLK) // MODC
@@ -250,12 +245,12 @@
         value = None
         for source in range(first, last + 1):
             at = source * MODC - tile * BLK
-            piece = mod_all[source]
+            piece = mod_z[source % NSEQ // NX, source % NX, source // NSEQ]
             if at % BLK:
                 piece = pltpu.roll(piece, at % BLK, 1)
             value = piece if value is None else jnp.where(lane_row >= at, piece, value)
         mod_rows[tile // 9, :, (tile % 9) * BLK : (tile % 9 + 1) * BLK] = value
-    hid0[...] = embed(j * 4, 4)
+    hid0[...] = embed(j)
 
     w_relay.wait_recv()
     w_forwards.append(remote(w_part(across, g), w_part(across, g), wf_s.at[2], wf_r.at[2], (other, y, s)))
@@ -384,6 +379,33 @@
             def _():
                 pltpu.make_async_copy(predsend.at[gg * NREQ + i], pred_in.at[slot], pr_r).start()
 
+    wait_bytes(pred_in, pr_r)
+    wait_bytes(stat_in.at[pl.ds(0, NSEQ - 1)], st_r)
+    pred_out[...] = pred_in[...]
+    stat_out[...] = stat_in[...]
+
+    wait_bytes(mod_y.at[pl.ds(0, NREQ - 1)], my_s)
+    wait_bytes(mod_x.at[pl.ds(0, NX - 1)], mx_s2)
+    wait_bytes(mod_z.at[pl.ds(0, NZ - 1)], mz_s)
+    wait_bytes(patch_x.at[pl.ds(0, NX - 1)], px_s)
+    wait_bytes(patch_z.at[pl.ds(0, NZ - 1)], pz_s)
+    wait_bytes(mixin.at[pl.ds(0, GROUP - 1)], mx_s)
+    wait_bytes(stat_in.at[pl.ds(0, NSEQ - 1)], st_s)
+    for i in range(2):
+        wait_bytes(w_part(0, 0), w_s.at[i])
+    for c in [w_relay, o_relay] + w_forwards + o_copies + o_forwards:
+        c.wait_send()
+    for self_copy, c in p_copies:
+
+        @pl.when(jnp.logical_not(self_copy))
+        def _():
+            c.wait_send()
+
+
+def finish(len_ref, step_ref, patches_ref, noise_ref, pred_ref, stat_ref, guided_out, norm_out, top_out):
+    g = lax.axis_index("cfg")
+    y = lax.axis_index("req")
+    s = lax.axis_index("seq")
     shape = (NREQ, 8, SLOT)
     which = lax.broadcasted_iota(jnp.int32, shape, 0)
     steps = jnp.zeros(shape, jnp.int32)
@@ -393,37 +415,19 @@
         limits = jnp.where(which == r, len_ref[y * NREQ + r], limits)
     valid = s * SLOT + lax.broadcasted_iota(jnp.int32, shape, 2) < limits
     channels = pl.ds(pl.multiple_of(g * 8, 8), 8)
-    own_patches = patches_ref[:, channels, :]
-    own_noise = noise_ref[:, channels, :]
-    finish = sampler_plan(own_patches, own_noise, steps.astype(jnp.float32), valid)
-
-    wait_bytes(pred_in, pr_r)
-    eps_cond, eps_uncond = pred_in[:NREQ, :8, :], pred_in[NREQ:, :8, :]
+    eps_cond, eps_uncond = pred_ref[:NREQ, :8, :], pred_ref[NREQ:, :8, :]
     guided = eps_uncond + guide_scale * (eps_cond - eps_uncond)
-    guided_out[...] = finish(guided, pred_in[:NREQ, 8:, :])
-
-    wait_bytes(stat_in.at[pl.ds(0, NSEQ - 1)], st_r)
+    guided_out[...] = sampler_step(
+        patches_ref[:, channels, :], noise_ref[:, channels, :], guided, pred_ref[:NREQ, 8:, :],
+        steps.astype(jnp.float32), valid,
+    )
     for r in range(NREQ):
-        row = stat_in[r * GROUP]
+        row = stat_ref[r * GROUP]
         for i in range(1, GROUP):
-            row = row + stat_in[r * GROUP + i]
+            row = row + stat_ref[r * GROUP + i]
         top_out[r : r + 1, :] = row[:, :HEADS]
         count = jnp.full((1, 1), len_ref[y * NREQ + r], jnp.int32).astype(jnp.float32) * D
         norm_out[:, r : r + 1] = jnp.sqrt(row[:, HEADS : HEADS + 1] / count)
-
-    wait_bytes(mod_all.at[pl.ds(0, NDEV - 1)], mod_s)
-    wait_bytes(patch_all.at[pl.ds(0, NSEQ - 1)], pat_s)
-    wait_bytes(mixin.at[pl.ds(0, GROUP - 1)], mx_s)
-    wait_bytes(stat_in.at[pl.ds(0, NSEQ - 1)], st_s)
-    for i in range(2):
-        wait_bytes(w_part(0, 0), w_s.at[i])
-    for c in [w_relay, o_relay] + w_forwards + o_copies + o_forwards:
-        c.wait_send()
-    for self_copy, c in p_copies:
-
-        @pl.when(jnp.logical_not(self_copy))
-        def _():
-            c.wait_send()
 
 
 def body(
@@ -435,24 +439,28 @@
     bf, f32 = jnp.bfloat16, jnp.float32
     dma = pltpu.SemaphoreType.DMA
     rates = np.exp(-math.log(10000.0) * np.arange(FREQ // 2) / (FREQ // 2)).astype(np.float32)[None, :]
-    guided, norms, top = pl.pallas_call(
+    patches_t, noise_t = jnp.transpose(patches, (0, 2, 1)), jnp.transpose(noise, (0, 2, 1))
+    pred, stats = pl.pallas_call(
         kernel,
         out_shape=(
-            jax.ShapeDtypeStruct((NREQ, 8, SLOT), f32),
-            jax.ShapeDtypeStruct((1, NREQ), f32),
-            jax.ShapeDtypeStruct((NREQ, HEADS), f32),
+            jax.ShapeDtypeStruct((8, 16, SLOT), f32),
+            jax.ShapeDtypeStruct((NSEQ, 1, BLK), f32),
         ),
-        in_specs=[smem] * 3 + [vmem] * 2 + [hbm] * 4 + [vmem] + [hbm] * 2 + [vmem] * 6,
-        out_specs=(vmem, vmem, vmem),
+        in_specs=[smem] * 3 + [vmem] + [hbm] * 4 + [vmem] + [hbm] * 2 + [vmem] * 6,
+        out_specs=(vmem, vmem),
         scratch_shapes=[
             pltpu.VMEM((FREQ, D), bf),
             pltpu.VMEM((D, D), bf),
             pltpu.VMEM((1001, D), bf),
             pltpu.VMEM((MODC, D), bf),
             pltpu.VMEM((16, 1, BLK), f32),
-            pltpu.VMEM((4, SLOT, 16), bf),
-            pltpu.VMEM((NSEQ, SLOT, 16), bf),
-            pltpu.VMEM((NDEV, 1, BLK), f32),
+            pltpu.VMEM((NREQ, 16, SLOT), bf),
+            pltpu.VMEM((NX, NREQ, 16, SLOT), bf),
+            pltpu.VMEM((NREQ, 16, BLK), bf),
+            pltpu.VMEM((NZ, 16, BLK), bf),
+            pltpu.VMEM((NREQ, NREQ, 1, BLK), f32),
+            pltpu.VMEM((NREQ, NX, NREQ, 1, BLK), f32),
+            pltpu.VMEM((NZ, NX, NREQ, 1, BLK), f32),
             pltpu.VMEM((5, 1, D), f32),
             pltpu.VMEM((SEQ_TOTAL, D), f32),
             pltpu.VMEM((BLK, D), f32),
@@ -468,7 +476,7 @@
             pltpu.VMEM((1, BLK), f32),
             pltpu.VMEM((NSEQ, 1, BLK), f32),
             pltpu.VMEM((2, 1, 1), f32),
-            dma((4,)), dma, dma, dma, dma,
+            dma((4,)), dma, dma, dma, dma, dma, dma, dma, dma, dma, dma,
             dma((3,)), dma((3,)), dma((3,)), dma((3,)), dma((3,)),
             dma((3,)), dma((3,)), dma, dma((3,)), dma((3,)),
             dma, dma, dma((8,)), dma, dma, dma,
@@ -479,10 +487,20 @@
         name="guided_block",
     )(
         lengths, timesteps, labels,
-        jnp.transpose(patches, (0, 2, 1)), jnp.transpose(noise, (0, 2, 1)),
-        time_w1, time_w2, label_table, jnp.transpose(mod_w), jnp.asarray(rates), qkv_w, jnp.transpose(out_w),
+        patches_t, time_w1, time_w2, label_table, jnp.transpose(mod_w), jnp.asarray(rates), qkv_w, jnp.transpose(out_w),
         jnp.transpose(head_w), patch_w, *position_factors(),
     )
+    guided, norms, top = pl.pallas_call(
+        finish,
+        out_shape=(
+            jax.ShapeDtypeStruct((NREQ, 8, SLOT), f32),
+            jax.ShapeDtypeStruct((1, NREQ), f32),
+            jax.ShapeDtypeStruct((NREQ, HEADS), f32),
+        ),
+        in_specs=[smem] * 2 + [vmem] * 4,
+        out_specs=(vmem, vmem, vmem),
+        name="guided_finish",
+    )(lengths, timesteps, patches_t, noise_t, pred, stats)
     return (jnp.transpose(guided, (0, 2, 1)), norms, top[None, :, :])
 
 

time: 63.7 us -> 54.6 us (0.86)
  Pallas kernels: 59.1 us -> 53.8 us
  local copies, waits for them, and re-layouts: 3.73 us -> 0 us
    pallas_call x1 -> x2, Pallas kernels: 59.1 us -> 53.8 us  [the longest x1 52.1 us: body(): pl.pallas_call(kernel, out_shape=(jax.ShapeDtypeStruct((8, 16, SLOT), f32...]
    unnamed x3 -> x0, local copies, waits for them, and re-layouts: 3.73 us -> none
where the time goes in v3:
time: 54.6 us; the launch traced here: 54.5 us
  Pallas kernels  53.8 us (99%)
  between operations  0.64 us (1%)
    pallas_call x1, Pallas kernels, body(): pl.pallas_call(kernel, out_shape=(jax.ShapeDtypeStruct((8, 16, SLOT), f32...  52.1 us
    pallas_call x1, Pallas kernels, body(): pl.pallas_call(finish, out_shape=(jax.ShapeDtypeStruct((NREQ, 8, SLOT), f...  1.69 us

profile of v3, /device:TPU:1, one launch (start us, length us, event | category | flops | bytes accessed | tf_op | source)
XLA Modules:
  0.0 54.5 jit_solution(3038075933467496738)
XLA Ops:
  0.6 52.1 %guided_block.1 = (f32[8,16,32]{2,1,0:T(8,128)}, f32[32,1,128]{2,1,0:T(1,128)}) custom-call(s32[16]{0:T(128)} %len_ref.3, s32[16]{0:T(128)} %step_ref.3, s32[16]{0:T(128)} %label_ref.1, f32[4,16,32]{2,1,0:T(8,128)} %bitcast.8, bf16[256,1152]{1,0:T(8,128)(2,1)} %w1_hbm.1, bf16[1152,1152]{1,0:T(8,128)(2,1)} %w2_hbm.1, bf16[1001,1152]{1,0:T(8,128)(2,1)} %table_hbm.1, ...), custom_call_target="tpu_custom_call" | custom-call | tf_op jit(solution)/shard_map/guided_block/pallas_call | solution.py:443
  52.8 1.7 %guided_finish.1 = (f32[4,8,32]{2,1,0:T(8,128)}, f32[1,4]{1,0:T(1,128)}, f32[4,16]{1,0:T(4,128)}) custom-call(s32[16]{0:T(128)} %len_ref.3, s32[16]{0:T(128)} %step_ref.3, f32[4,16,32]{2,1,0:T(8,128)} %bitcast.9, f32[4,16,32]{2,1,0:T(8,128)} %bitcast.12, f32[8,16,32]{2,1,0:T(8,128)} %get-tuple-element.8.pred_ref, f32[32,1,128]{2,1,0:T(1,128)} %get-tuple-element.9.stat_ref), custom_call_target="tpu_custom_call" | custom-call | tf_op jit(solution)/shard_map/guided_finish/pallas_call | solution.py:493
